TPU v7x, 512 devices: a whole 4x4x16 slice. The times are simulated.
512 devices in a mesh: dp: 16 (over z), seq: 8 (over x, core), index: 4 (over y).
Axes of the slice: x: 4, y: 4, z: 16, core: 2. Of those that a mesh axis runs over, the one named last changes fastest.
Arguments:
- hidden: bfloat16 [16, 2048, 2048], P('dp', 'seq'), may hold values from -32 to 32
- proj_weight: bfloat16 [4, 2048, 1536], P(None, 'dp', 'index')
- stretch_lengths: int32 [16, 32], P('dp'), may hold values from 1 to 512, 2048 in all within a row
- shard_of: int32 [16, 32, 1], P('dp', 'seq'), may hold values from 0 to 3; in each aligned block of 4 rows (0 to 3, 4 to 7, ..., all dimensions but the last counted through in order) at most 2 rows name the same one
Outputs:
- layer_out: bfloat16 [16, 2048, 2048], P('dp', 'seq', 'index')
- shelf: float32 [16, 8, 4, 2, 2048], P('dp', 'seq', 'index')
Inputs may be any that keep to these rules, and one draw needn't show every extreme that they name: `stretch_lengths`: the 32 lengths of a manual sum to 2048; the largest is 512. `shard_of`: in each aligned block of 4 rows of a manual no shard is named more than 2 times, a bound that some block reaches.
All inputs are finite; a program needn't handle non-finite values.
Results may differ from a plain program's by a relative error of at most 0.01.
Values may be sent and summed in bfloat16 or wider, within the bound.
A program may use at most 64 MiB of HBM per device.

v0:
```python
import jax
import jax.numpy as jnp
from jax import lax
from jax.sharding import PartitionSpec as P

D = 2048
HD = 64
HALF_WIN = 256


def with_halo(cells, sides, width):
    for axis, dim in sides:
        count = lax.axis_size(axis)
        ends = count - 1
        head = lax.slice_in_dim(cells, 0, width, axis=dim)
        tail = lax.slice_in_dim(cells, cells.shape[dim] - width, cells.shape[dim], axis=dim)
        cells = jnp.concatenate(
            [
                lax.ppermute(tail, axis, [(i, (i + 1) % count) for i in range(ends)]),
                cells,
                lax.ppermute(head, axis, [((i + 1) % count, i) for i in range(ends)]),
            ],
            axis=dim,
        )
    return cells


def rotate(values_in, positions):
    half_dim = HD // 2
    freqs = 10000.0 ** (-2.0 * jnp.arange(half_dim, dtype=jnp.float32) / HD)
    angles = positions.astype(jnp.float32)[:, None] * freqs[None, :]
    cosine = jnp.cos(angles)[:, None, :]
    sine = jnp.sin(angles)[:, None, :]
    first = values_in[..., :half_dim]
    second = values_in[..., half_dim:]
    return jnp.concatenate([first * cosine - second * sine, second * cosine + first * sine], -1)


def window_heads(queries, key_rows, value_rows, visible):
    scale = HD ** (-0.5)

    def one_head(items):
        query_head, key_head, value_head = items
        scores = jnp.dot(query_head, key_head.T, preferred_element_type=jnp.float32) * scale
        scores = jnp.where(visible, scores, -1e30)
        maxima = jnp.max(scores, -1, keepdims=True)
        expo = jnp.exp(scores - maxima)
        weights = (expo / jnp.sum(expo, -1, keepdims=True)).astype(jnp.bfloat16)
        return jnp.dot(weights, value_head, preferred_element_type=jnp.float32).astype(jnp.bfloat16)

    context = lax.map(
        one_head,
        (jnp.moveaxis(queries, 1, 0), jnp.moveaxis(key_rows, 1, 0), jnp.moveaxis(value_rows, 1, 0)),
    )
    return jnp.moveaxis(context, 0, 1)


def body(hidden, proj_weight, stretch_lengths, shard_of):
    states = hidden[0]
    tokens_here = states.shape[0]
    width = proj_weight.shape[2]
    heads_here = width // HD
    seq_index = lax.axis_index("seq")
    group_index = lax.axis_index("index")
    seq_count = lax.axis_size("seq")
    index_count = lax.axis_size("index")
    total_length = tokens_here * seq_count
    positions = seq_index * tokens_here + jnp.arange(tokens_here, dtype=jnp.int32)
    shard_rows = lax.all_gather(proj_weight, "dp", axis=1, tiled=True)
    projected = jnp.einsum(
        "td,jdc->jtc", states, shard_rows[:3], preferred_element_type=jnp.float32
    )
    out_rows_full = shard_rows[3]
    queries = rotate(projected[0].reshape(tokens_here, heads_here, HD), positions).astype(
        jnp.bfloat16
    )
    key_rows = rotate(projected[1].reshape(tokens_here, heads_here, HD), positions).astype(
        jnp.bfloat16
    )
    value_rows = projected[2].astype(jnp.bfloat16)
    stacked = jnp.stack([key_rows.reshape(tokens_here, width), value_rows])
    padded = with_halo(stacked, (("seq", 1),), HALF_WIN)
    span = tokens_here + 2 * HALF_WIN
    key_part = padded[0, 0:span].reshape(span, heads_here, HD)
    value_part = padded[1, 0:span].reshape(span, heads_here, HD)
    key_pos = seq_index * tokens_here + 0 - HALF_WIN + jnp.arange(span, dtype=jnp.int32)
    visible = (
        (jnp.abs(key_pos[None, :] - positions[:, None]) <= HALF_WIN)
        & (key_pos[None, :] >= 0)
        & (key_pos[None, :] < total_length)
    )
    context_parts = window_heads(queries, key_part, value_part, visible).reshape(tokens_here, width)
    partial_value = lax.dot_general(
        context_parts, out_rows_full, (((1,), (1,)), ((), ())), preferred_element_type=jnp.float32
    )
    lengths = stretch_lengths[0]
    stretch_count = lengths.shape[0]
    per_block = stretch_count // seq_count
    ends = jnp.cumsum(lengths, dtype=jnp.int32)
    starts = ends - lengths
    row_ids = jnp.arange(stretch_count, dtype=jnp.int32)
    order = row_ids % per_block * seq_count + row_ids // per_block
    row_starts = starts[order]
    row_ends = ends[order]
    member = (
        (positions[None, :] >= row_starts[:, None]) & (positions[None, :] < row_ends[:, None])
    ).astype(jnp.bfloat16)
    shard_ids = shard_of[0, :, 0]
    local_rows = jnp.arange(per_block, dtype=jnp.int32)
    earlier = (shard_ids[:, None] == shard_ids[None, :]) & (
        local_rows[None, :] < local_rows[:, None]
    )
    slot_rank = jnp.sum(earlier.astype(jnp.int32), 1)
    capacity = per_block // 2
    slot_ids = jnp.arange(capacity, dtype=jnp.int32)
    quarter = D // index_count
    summed = lax.psum_scatter(
        partial_value.astype(jnp.bfloat16), "index", scatter_dimension=1, tiled=True
    ).astype(jnp.float32)
    own_states = lax.dynamic_slice_in_dim(states, group_index * quarter, quarter, 1)
    layer = (own_states.astype(jnp.float32) + summed).astype(jnp.bfloat16)
    partial_pool = jnp.dot(member, layer, preferred_element_type=jnp.float32)
    pooled = lax.psum_scatter(
        partial_pool.astype(jnp.bfloat16), "seq", scatter_dimension=0, tiled=True
    ).astype(jnp.float32)
    shard_range = jnp.arange(index_count, dtype=jnp.int32)
    routing = (
        (shard_ids[None, None, :] == shard_range[:, None, None])
        & (slot_rank[None, None, :] == slot_ids[None, :, None])
    ).astype(jnp.float32)
    outgoing = jnp.einsum("rkc,cf->rkf", routing, pooled, precision=lax.Precision.HIGHEST)
    arrived = lax.all_to_all(outgoing, "index", split_axis=0, concat_axis=2, tiled=True)[0]
    shelf_rows = arrived * lax.rsqrt(jnp.mean(arrived * arrived, -1, keepdims=True) + 1e-06)
    return (layer[None], shelf_rows[None, None, None])


def solution(mesh):
    in_specs = (P("dp", "seq", None), P(None, "dp", "index"), P("dp", None), P("dp", "seq", None))
    out_specs = (P("dp", "seq", "index"), P("dp", "seq", "index", None, None))
    return jax.shard_map(body, mesh=mesh, in_specs=in_specs, out_specs=out_specs, check_vma=False)
```

profile of v0, /device:TPU:1, one launch (start us, length us, event | category | flops | bytes accessed | tf_op | source)
XLA Modules:
  0.0 224.0 jit_solution(12025470082465413667)
XLA Ops:
  7.2 0.0 all-gather.2.cloned.1.call-start
  7.2 1.9 copy.24
  9.2 0.0 all-gather.2.cloned.1.call-update
  9.2 0.0 reduce-scatter.2.cloned.1.call-start
  9.3 1.2 multiply_cosine_fusion
  10.5 105.8 %all-gather.2.cloned.1.call-done = bf16[4,2048,384]{1,2,0:T(8,128)(2,1)} async-done(((bf16[4,128,384]{1,2,0:T(8,128)(2,1)}), bf16[4,2048,384]{1,2,0:T(8,128)(2,1)}) %all-gather.2.cloned.1.call-update) | async-done | bytes 6291472 | tf_op jit(solution)/shard_map/all_gather | solution.py:69
  116.2 4.1 %convolution_bitcast_fusion = f32[3,256,384]{1,2,0:T(8,128)S(1)} fusion(bf16[4,2048,384]{1,2,0:T(8,128)(2,1)} %all-gather.2.cloned.1.call-done, bf16[1,256,2048]{2,1,0:T(8,128)(2,1)} %param.6), kind=kOutput, calls=%fused_computation.24 | convolution fusion | flops 1207959552 | bytes 8519680 | tf_op jit(solution)/shard_map/td,jdc->jtc/dot_general | solution.py:70
  120.4 0.1 fusion.40
  120.5 0.3 copy.39
  120.8 0.3 copy.37
  121.0 0.3 copy.38
  121.3 0.3 copy.36
  121.6 1.4 subtract_convert_fusion
  123.0 0.4 maximum_bitcast_fusion
  123.5 0.2 copy.29
  123.7 14.2 %collective-permute-start.1 = (bf16[2,256,384]{1,2,0:T(8,128)(2,1)S(1)}, bf16[2,256,384]{1,2,0:T(8,128)(2,1)S(1)}, u32[]{:S(2)}, u32[]{:S(2)}) collective-permute-start(bf16[2,256,384]{1,2,0:T(8,128)(2,1)S(1)} %pad_maximum_fusion.2), channel_id=1, source_target_pairs={{4,0},{8,4},{12,8},{16,12},{20,16},{24,20},{28,24},{5,1},{9,5},{13... | collective-permute-start | bytes 1179656 | tf_op jit(solution)/shard_map/ppermute | solution.py:21
  137.9 3.0 %collective-permute-start = (bf16[2,256,384]{1,2,0:T(8,128)(2,1)S(1)}, bf16[2,256,384]{1,2,0:T(8,128)(2,1)S(1)}, u32[]{:S(2)}, u32[]{:S(2)}) collective-permute-start(bf16[2,256,384]{1,2,0:T(8,128)(2,1)S(1)} %pad_maximum_fusion.2), channel_id=1, source_target_pairs={{0,4},{4,8},{8,12},{12,16},{16,20},{20,24},{24,28},{1,5},{5,9},{9,... | collective-permute-start | bytes 1179656 | tf_op jit(solution)/shard_map/ppermute | solution.py:19
  140.9 3.5 %collective-permute-done.1 = bf16[2,256,384]{1,2,0:T(8,128)(2,1)S(1)} collective-permute-done((bf16[2,256,384]{1,2,0:T(8,128)(2,1)S(1)}, bf16[2,256,384]{1,2,0:T(8,128)(2,1)S(1)}, u32[]{:S(2)}, u32[]{:S(2)}) %collective-permute-start.1) | collective-permute-done | bytes 393248 | tf_op jit(solution)/shard_map/ppermute | solution.py:21
  144.4 1.2 collective-permute-done
  145.6 0.1 pad_maximum_fusion
  145.7 0.1 fusion.39
  145.8 0.7 copy.30
  146.5 0.7 copy.31
  147.2 7.3 %while.11 = (s32[]{:T(128)}, bf16[6,256,64]{1,2,0:T(8,128)(2,1)S(1)}, bf16[6,256,64]{2,1,0:T(8,128)(2,1)S(1)}, bf16[6,768,64]{2,1,0:T(8,128)(2,1)S(1)}, bf16[6,7...) while((s32[]{:T(128)}, ...), condition=%wide.region_3.4_spmd.clone, body=%wide.region_0.3_spmd.clone.sunk | while | flops 52903424 | bytes 2865261 | solution.py:51
  147.3 0.5 fusion.50
  147.8 0.3 fusion.51
  148.1 0.4 fusion.52
  148.4 0.5 fusion.50
  149.0 0.3 fusion.51
  149.3 0.4 fusion.52
  149.7 0.5 fusion.50
  150.2 0.3 fusion.51
  150.5 0.4 fusion.52
  150.9 0.5 fusion.50
  151.4 0.3 fusion.51
  151.7 0.4 fusion.52
  152.1 0.5 fusion.50
  152.6 0.3 fusion.51
  152.9 0.4 fusion.52
  153.3 0.5 fusion.50
  153.8 0.3 fusion.51
  154.1 0.4 fusion.52
  154.5 0.0 copy-start.1
  154.5 3.2 %convolution_convert_fusion.1 = bf16[256,2048]{1,0:T(8,128)(2,1)} fusion(bf16[256,384]{0,1:T(8,128)(2,1)S(1)} %bitcast.86, bf16[4,2048,384]{1,2,0:T(8,128)(2,1)} %all-gather.2.cloned.1.call-done), kind=kOutput, calls=%fused_computation.22 | convolution fusion | flops 403177472 | bytes 2818048 | tf_op jit(solution)/shard_map/dot_general | solution.py:93
  157.7 0.0 reduce-scatter.2.cloned.1.call-update
  157.7 0.0 copy-done.1
  157.7 0.1 copy.32
  157.8 0.1 reduce-window.9
  157.9 0.1 reduce.1
  158.0 0.7 gather_fusion.1
  158.7 0.7 gather_fusion
  159.4 1.3 dynamic-slice.1
  161.4 0.0 copy-done.2
  161.4 0.2 convert_reduce_fusion
  161.6 22.7 %reduce-scatter.2.cloned.1.call-done = bf16[256,512]{1,0:T(8,128)(2,1)} async-done(((bf16[256,2048]{1,0:T(8,128)(2,1)}), bf16[256,512]{1,0:T(8,128)(2,1)}) %reduce-scatter.2.cloned.1.call-update) | async-done | bytes 262160 | tf_op jit(solution)/shard_map/reduce_scatter | solution.py:117
  184.3 0.0 copy-done
  184.3 1.1 convolution_convert_fusion.2
  185.5 22.7 %all-reduce = bf16[32,512]{1,0:T(8,128)(2,1)S(1)} all-reduce(bf16[32,512]{1,0:T(8,128)(2,1)S(1)} %convolution_convert_fusion.2), channel_id=3, replica_groups=mesh['dp'=16,'seq'=8,'index'=4] {'seq'}, use_global_device_ids=true, to_apply=%region_7.8.clone | all-reduce | flops 16384 | bytes 65536
  208.2 0.7 fusion.27
  208.9 3.3 %all-to-all-start = ((f32[4,2,512]{2,1,0:T(2,128)}), f32[4,2,512]{2,1,0:T(2,128)S(1)}, u32[]{:S(2)}, u32[]{:S(2)}) async-start(f32[4,2,512]{2,1,0:T(2,128)} %fusion.27), calls=%async_computation.1 | async-start | bytes 32768 | tf_op jit(solution)/shard_map/all_to_all | solution.py:132
  212.2 1.7 fusion.19
  213.9 2.4 %all-to-all-done = f32[4,2,512]{2,1,0:T(2,128)S(1)} async-done(((f32[4,2,512]{2,1,0:T(2,128)}), f32[4,2,512]{2,1,0:T(2,128)S(1)}, u32[]{:S(2)}, u32[]{:S(2)}) %all-to-all-start) | async-done | bytes 16416 | tf_op jit(solution)/shard_map/all_to_all | solution.py:132
  216.3 0.1 fusion.23
  216.5 0.7 broadcast_multiply_fusion
  (19 shorter events, 0.2 us)
Async XLA Ops:
  7.2 109.1 %all-gather.2.cloned.1.call-start = ((), (), s32[]{:S(2)}) async-start(), calls=%async_computation.2 | async-start | bytes 6684672 | tf_op jit(solution)/shard_map/all_gather | solution.py:69
  9.2 175.1 %reduce-scatter.2.cloned.1.call-start = ((), (), s32[]{:S(2)}) async-start(), calls=%async_computation.3 | async-start | bytes 1310720 | tf_op jit(solution)/shard_map/reduce_scatter | solution.py:117
  123.7 20.7 %collective-permute-start.1 = (bf16[2,256,384]{1,2,0:T(8,128)(2,1)S(1)}, bf16[2,256,384]{1,2,0:T(8,128)(2,1)S(1)}, u32[]{:S(2)}, u32[]{:S(2)}) collective-permute-start(bf16[2,256,384]{1,2,0:T(8,128)(2,1)S(1)} %pad_maximum_fusion.2), channel_id=1, source_target_pairs={{4,0},{8,4},{12,8},{16,12},{20,16},{24,20},{28,24},{5,1},{9,5},{13... | collective-permute-start | bytes 1179656 | tf_op jit(solution)/shard_map/ppermute | solution.py:21
  137.9 7.7 %collective-permute-start = (bf16[2,256,384]{1,2,0:T(8,128)(2,1)S(1)}, bf16[2,256,384]{1,2,0:T(8,128)(2,1)S(1)}, u32[]{:S(2)}, u32[]{:S(2)}) collective-permute-start(bf16[2,256,384]{1,2,0:T(8,128)(2,1)S(1)} %pad_maximum_fusion.2), channel_id=1, source_target_pairs={{0,4},{4,8},{8,12},{12,16},{16,20},{20,24},{24,28},{1,5},{5,9},{9,... | collective-permute-start | bytes 1179656 | tf_op jit(solution)/shard_map/ppermute | solution.py:19
  154.5 3.2 %copy-start.1 = (s32[1,32]{1,0:T(1,128)S(1)}, s32[1,32]{1,0:T(1,128)}, u32[]{:S(2)}) copy-start(s32[1,32]{1,0:T(1,128)} %param.8) | copy-start | bytes 388
  157.7 3.7 %copy-start.2 = (s32[1,4,1]{1,2,0:T(1,128)S(1)}, s32[1,4,1]{1,2,0:T(1,128)}, u32[]{:S(2)}) copy-start(s32[1,4,1]{1,2,0:T(1,128)} %param.9) | copy-start | bytes 52
  157.7 26.6 %copy-start = (bf16[1,256,2048]{2,1,0:T(8,128)(2,1)S(1)}, bf16[1,256,2048]{2,1,0:T(8,128)(2,1)}, u32[]{:S(2)}) copy-start(bf16[1,256,2048]{2,1,0:T(8,128)(2,1)} %param.6) | copy-start | bytes 3145732
  208.9 7.4 %all-to-all-start = ((f32[4,2,512]{2,1,0:T(2,128)}), f32[4,2,512]{2,1,0:T(2,128)S(1)}, u32[]{:S(2)}, u32[]{:S(2)}) async-start(f32[4,2,512]{2,1,0:T(2,128)} %fusion.27), calls=%async_computation.1 | async-start | bytes 32768 | tf_op jit(solution)/shard_map/all_to_all | solution.py:132
Sparse Core Ops, SparseCore 0:
  10.0 106.2 all-gather.1
  157.8 26.4 reduce-scatter.1
where the time goes:
time: 227 us; the launch traced here: 224 us
  waiting for transfers between devices  136 us (60%)
  blocking collectives  22.7 us (10%)
  starting transfers between devices  20.5 us (9%)
  between operations  15 us (7%)
  matrix products  14.7 us (6%)
  other arithmetic  7.88 us (3%)
  local copies, waits for them, and re-layouts  7.61 us (3%)
    all_gather x1, waiting for transfers between devices, body(): shard_rows = lax.all_gather(proj_weight, 'dp', axis=1, tiled=True)  106 us
    reduce_scatter x1, waiting for transfers between devices, body(): lax.psum_scatter(partial_value.astype(jnp.bfloat16), 'index', scatter_dim...  22.7 us
    unnamed x1, blocking collectives  22.7 us
    ppermute x1, starting transfers between devices, with_halo(): lax.ppermute(head, axis, [((i + 1) % count, i) for i in range(ends)])  14.2 us
  transfers between devices with their start and end apart: 5, of which 5 were waited for; matrix products, arithmetic and copies ran while one was open for 3% of the time, Pallas kernels for 0%

commit v1 on v0

--- a/solution.py
+++ b/solution.py
@@ -1,11 +1,210 @@
+import functools
+
 import jax
 import jax.numpy as jnp
 from jax import lax
+from jax.experimental import pallas as pl
+from jax.experimental.pallas import tpu as pltpu
 from jax.sharding import PartitionSpec as P
 
 D = 2048
 HD = 64
 HALF_WIN = 256
+MESH = pl.DeviceIdType.MESH
+VMEM = pltpu.VMEM
+
+
+def rope_tables(positions, lanes):
+    lane = jnp.arange(lanes, dtype=jnp.int32) % HD
+    half = HD // 2
+    freqs = 10000.0 ** (-2.0 * (lane % half).astype(jnp.float32) / HD)
+    angles = positions.astype(jnp.float32)[:, None] * freqs[None, :]
+    sign = jnp.where(lane < half, -1.0, 1.0).astype(jnp.float32)
+    return jnp.cos(angles), jnp.sin(angles) * sign[None, :]
+
+
+def gather_kernel(x_ref, w_ref, cos_ref, sin_ref, q_ref, k_ref, v_ref, o_ref,
+                  w_all, acc, local_sem, zs, zr, xs, xr, ps, pr):
+    nz = lax.axis_size("dp")
+    ns = lax.axis_size("seq")
+    z = lax.axis_index("dp")
+    s = lax.axis_index("seq")
+    half = nz // 2
+    rows = w_ref.shape[1]
+    pieces = w_ref.shape[0]
+    core = lax.rem(s, 2)
+    par = lax.rem(s // 2, 2)
+    partner = s + 1 - 2 * core
+    up = {"dp": lax.rem(z + 1, nz)}
+    down = {"dp": lax.rem(z + nz - 1, nz)}
+    right = {"seq": lax.rem(s + 2, ns)}
+    left = {"seq": lax.rem(s + ns - 2, ns)}
+    mate = {"seq": partner}
+
+    barrier = pltpu.get_barrier_semaphore()
+    for peer in (up, down, right, left, mate):
+        pl.semaphore_signal(barrier, inc=1, device_id=peer, device_id_type=MESH)
+    pl.semaphore_wait(barrier, 5)
+
+    part = rows // 4
+    sub = part // 2
+    mine = pl.multiple_of(rows // 2 * par + part * core, 16)
+    other = pl.multiple_of(rows // 2 * (1 - par) + part * core, 16)
+
+    def remote(src, dst, send, recv, device):
+        return pltpu.make_async_remote_copy(src_ref=src, dst_ref=dst, send_sem=send, recv_sem=recv,
+                                            device_id=device, device_id_type=MESH)
+
+    def z_copy(g, o, slot, device, first=False):
+        ref = w_all.at[o, g, pl.ds(mine, part)]
+        src = w_ref.at[g, pl.ds(mine, part)] if first else ref
+        return remote(src, ref, zs.at[g, slot], zr.at[g, o], device)
+
+    def z_wait(g, o):
+        z_copy(g, o, o, up).wait_recv()
+
+    def x_copy(o, which):
+        ref = w_all.at[o, :, pl.ds(mine + which * sub, sub)]
+        return remote(ref, ref, xs.at[which, o], xr.at[which, o], (right, left)[which])
+
+    def x_wait(o, which):
+        ref = w_all.at[o, :, pl.ds(other + which * sub, sub)]
+        remote(ref, ref, xs.at[which, o], xr.at[which, o], right).wait_recv()
+
+    def p_copy(o, which):
+        start = (mine, other)[which]
+        ref = w_all.at[o, :, pl.ds(start, part)]
+        return remote(ref, ref, ps.at[which, o], pr.at[which, o], mate)
+
+    def p_wait(o, which):
+        start = pl.multiple_of(rows // 2 * ((par, 1 - par)[which]) + part * (1 - core), 16)
+        ref = w_all.at[o, :, pl.ds(start, part)]
+        remote(ref, ref, ps.at[which, o], pr.at[which, o], mate).wait_recv()
+
+    def minus(k):
+        return lax.rem(z + nz - k, nz)
+
+    def plus(k):
+        return lax.rem(z + k, nz)
+
+    for g in range(pieces):
+        z_copy(g, z, z, up, True).start()
+        z_copy(g, z, plus(half), down, True).start()
+    own = pltpu.make_async_copy(w_ref, w_all.at[z], local_sem)
+    own.start()
+    acc[...] = jnp.zeros_like(acc)
+    own.wait()
+
+    def arrive(o, k, last, device):
+        for g in range(pieces):
+            z_wait(g, o)
+
+            @pl.when(k < last)
+            def _():
+                z_copy(g, o, o, device).start()
+        for which in range(2):
+            x_copy(o, which).start()
+        p_copy(o, 0).start()
+
+    def cross(o):
+        for which in range(2):
+            x_wait(o, which)
+        p_copy(o, 1).start()
+
+    def multiply(a, b):
+        cols_a = pl.ds(pl.multiple_of(a * rows, 128), rows)
+        cols_b = pl.ds(pl.multiple_of(b * rows, 128), rows)
+        lhs = jnp.concatenate([x_ref[:, cols_a], x_ref[:, cols_b]], axis=1)
+        for j in range(3):
+            rhs = jnp.concatenate([w_all[a, j], w_all[b, j]], axis=0)
+            acc[j] += jnp.dot(lhs, rhs, preferred_element_type=jnp.float32)
+
+    def settle(o):
+        p_wait(o, 0)
+        p_wait(o, 1)
+
+    def step(k, carry):
+        arrive(minus(k), k, half, up)
+
+        @pl.when(k < half)
+        def _():
+            arrive(plus(k), k, half - 1, down)
+
+        @pl.when(k >= 2)
+        def _():
+            cross(minus(k - 1))
+            cross(plus(k - 1))
+
+        @pl.when(k >= 3)
+        def _():
+            a, b = minus(k - 2), plus(k - 2)
+            settle(a)
+            settle(b)
+            multiply(a, b)
+
+        return carry
+
+    lax.fori_loop(1, half + 1, step, 0)
+    cross(minus(half))
+    settle(minus(half - 1))
+    settle(plus(half - 1))
+    multiply(minus(half - 1), plus(half - 1))
+    settle(minus(half))
+    multiply(z, minus(half))
+
+    width = q_ref.shape[1]
+    lane = lax.broadcasted_iota(jnp.int32, (q_ref.shape[0], 128), 1)
+    lower = lax.rem(lane, HD) < HD // 2
+    for j, ref in ((0, q_ref), (1, k_ref)):
+        for start in range(0, width, 128):
+            value = acc[j, :, start:start + 128]
+            swapped = jnp.where(lower, pltpu.roll(value, 128 - HD // 2, 1), pltpu.roll(value, HD // 2, 1))
+            ref[:, start:start + 128] = (value * cos_ref[...] + swapped * sin_ref[...]).astype(jnp.bfloat16)
+    v_ref[...] = acc[2].astype(jnp.bfloat16)
+    o_ref[...] = w_all[:, 3]
+
+    def finish(k, carry):
+        a, b = minus(k), plus(k)
+        for g in range(pieces):
+            z_copy(g, a, a, up).wait_send()
+
+            @pl.when(k < half - 1)
+            def _():
+                z_copy(g, b, jnp.where(k == 0, plus(half), b), down).wait_send()
+        return carry
+
+    lax.fori_loop(0, half, finish, 0)
+
+    def finish_cross(k, carry):
+        o = plus(k)
+        for which in range(2):
+            x_copy(o, which).wait_send()
+            p_copy(o, which).wait_send()
+        return carry
+
+    lax.fori_loop(1, nz, finish_cross, 0)
+
+
+def gathered_projection(states, weights, cosine, sine):
+    tokens = states.shape[0]
+    pieces, rows, width = weights.shape
+    nz = lax.axis_size("dp")
+    out = jax.ShapeDtypeStruct((tokens, width), jnp.bfloat16)
+    dma = pltpu.SemaphoreType.DMA
+    return pl.pallas_call(
+        gather_kernel,
+        out_shape=(out, out, out, jax.ShapeDtypeStruct((nz, rows, width), jnp.bfloat16)),
+        in_specs=[pl.BlockSpec(memory_space=VMEM)] * 4,
+        out_specs=[pl.BlockSpec(memory_space=VMEM)] * 4,
+        scratch_shapes=[
+            VMEM((nz, pieces, rows, width), jnp.bfloat16),
+            VMEM((3, tokens, width), jnp.float32),
+            dma(()),
+            dma((pieces, nz)), dma((pieces, nz)),
+            dma((2, nz)), dma((2, nz)), dma((2, nz)), dma((2, nz)),
+        ],
+        compiler_params=pltpu.CompilerParams(collective_id=0, has_side_effects=True),
+    )(states, weights, cosine, sine)
 
 
 def with_halo(cells, sides, width):
@@ -25,17 +224,6 @@
     return cells
 
 
-def rotate(values_in, positions):
-    half_dim = HD // 2
-    freqs = 10000.0 ** (-2.0 * jnp.arange(half_dim, dtype=jnp.float32) / HD)
-    angles = positions.astype(jnp.float32)[:, None] * freqs[None, :]
-    cosine = jnp.cos(angles)[:, None, :]
-    sine = jnp.sin(angles)[:, None, :]
-    first = values_in[..., :half_dim]
-    second = values_in[..., half_dim:]
-    return jnp.concatenate([first * cosine - second * sine, second * cosine + first * sine], -1)
-
-
 def window_heads(queries, key_rows, value_rows, visible):
     scale = HD ** (-0.5)
 
@@ -66,19 +254,11 @@
     index_count = lax.axis_size("index")
     total_length = tokens_here * seq_count
     positions = seq_index * tokens_here + jnp.arange(tokens_here, dtype=jnp.int32)
-    shard_rows = lax.all_gather(proj_weight, "dp", axis=1, tiled=True)
-    projected = jnp.einsum(
-        "td,jdc->jtc", states, shard_rows[:3], preferred_element_type=jnp.float32
-    )
-    out_rows_full = shard_rows[3]
-    queries = rotate(projected[0].reshape(tokens_here, heads_here, HD), positions).astype(
-        jnp.bfloat16
-    )
-    key_rows = rotate(projected[1].reshape(tokens_here, heads_here, HD), positions).astype(
-        jnp.bfloat16
-    )
-    value_rows = projected[2].astype(jnp.bfloat16)
-    stacked = jnp.stack([key_rows.reshape(tokens_here, width), value_rows])
+    cosine, sine = rope_tables(positions, 128)
+    queries, keys, value_rows, out_rows = gathered_projection(states, proj_weight, cosine, sine)
+    out_rows_full = out_rows.reshape(-1, width)
+    queries = queries.reshape(tokens_here, heads_here, HD)
+    stacked = jnp.stack([keys, value_rows])
     padded = with_halo(stacked, (("seq", 1),), HALF_WIN)
     span = tokens_here + 2 * HALF_WIN
     key_part = padded[0, 0:span].reshape(span, heads_here, HD)

time: 227 us -> 151 us (0.67)
  the two profiles are of different devices: /device:TPU:1 before, /device:TPU:32 now
where the time goes in v1:
time: 151 us
  Pallas kernels  48 us (32%)
  waiting for transfers between devices  34.8 us (23%)
  blocking collectives  24.1 us (16%)
  between operations  14.9 us (10%)
  matrix products  9.16 us (6%)
  other arithmetic  8.12 us (5%)
  starting transfers between devices  7.44 us (5%)
  local copies, waits for them, and re-layouts  4.51 us (3%)
    pallas_call x1, Pallas kernels, gathered_projection(): pl.pallas_call(gather_kernel, out_shape=(out, out, out, jax.ShapeDtypeStr...  48 us
    reduce_scatter x1, waiting for transfers between devices, body(): lax.psum_scatter(partial_value.astype(jnp.bfloat16), 'index', scatter_dim...  30 us
    unnamed x1, blocking collectives  24.1 us
    all_to_all x1, waiting for transfers between devices, body(): lax.all_to_all(outgoing, 'index', split_axis=0, concat_axis=2, tiled=True)  3.59 us
    dot_general x6, matrix products, one_head(): jnp.dot(query_head, key_head.T, preferred_element_type=jnp.float32) * scale  3.36 us
    all_to_all x1, starting transfers between devices, body(): lax.all_to_all(outgoing, 'index', split_axis=0, concat_axis=2, tiled=True)  3.25 us
  transfers between devices with their start and end apart: 4, of which 3 were waited for; matrix products, arithmetic and copies ran while one was open for 4% of the time, Pallas kernels for 0%

profile of v1, /device:TPU:32, one launch (start us, length us, event | category | flops | bytes accessed | tf_op | source)
XLA Modules:
  0.0 151.0 jit_solution(17673088401963753460)
XLA Ops:
  7.2 0.0 reduce-scatter.2.cloned.1.call-start
  7.2 1.2 fusion.17
  8.5 48.0 %shard_map.59 = (bf16[256,384]{1,0:T(8,128)(2,1)}, bf16[256,384]{1,0:T(8,128)(2,1)}, bf16[256,384]{1,0:T(8,128)(2,1)}, bf16[16,128,384]{2,1,0:T(8,128)(2,1)}) custom-call(bf16[256,2048]{1,0:T(8,128)(2,1)} %bitcast.72, bf16[4,128,384]{2,1,0:T(8,128)(2,1)} %w_ref.1, f32[256,128]{1,0:T(8,128)} %get-tuple-element.108.cos_ref, f32[256,128]{1,0:T(8,128)} %get-tuple-element.107.sin_ref), custom_call_target="tpu_custom_call" | custom-call | tf_op jit(solution)/shard_map/pallas_call | solution.py:194
  56.5 1.1 pad_maximum_fusion.1
  57.5 2.9 %collective-permute-start = (bf16[2,256,384]{2,1,0:T(8,128)(2,1)S(1)}, bf16[2,256,384]{2,1,0:T(8,128)(2,1)S(1)}, u32[]{:S(2)}, u32[]{:S(2)}) collective-permute-start(bf16[2,256,384]{2,1,0:T(8,128)(2,1)S(1)} %pad_maximum_fusion.1), channel_id=1, source_target_pairs={{0,4},{4,8},{8,12},{12,16},{16,20},{20,24},{24,28},{1,5},{5,9},{9,... | collective-permute-start | bytes 1179656 | tf_op jit(solution)/shard_map/ppermute | solution.py:218
  60.4 1.3 collective-permute-start.1
  61.7 1.1 copy.17
  62.8 0.0 collective-permute-done
  62.8 1.2 collective-permute-done.1
  64.0 1.1 pad_maximum_fusion
  65.2 0.1 fusion.43
  65.3 0.3 copy.18
  65.5 0.3 copy.19
  65.8 0.0 copy-start.1
  65.8 7.2 %while.11 = (s32[]{:T(128)}, bf16[6,256,64]{1,2,0:T(8,128)(2,1)S(1)}, bf16[6,256,64]{1,2,0:T(8,128)(2,1)S(1)}, bf16[6,768,64]{1,2,0:T(8,128)(2,1)S(1)}, bf16[6,7...) while((s32[]{:T(128)}, ...), condition=%wide.region_3.4_spmd.clone, body=%wide.region_0.3_spmd.clone.sunk | while | flops 52903424 | bytes 2635877 | solution.py:239
  65.8 0.5 fusion.51
  66.4 0.3 fusion.52
  66.6 0.4 fusion.53
  67.0 0.6 fusion.51
  67.6 0.3 fusion.52
  67.9 0.4 fusion.53
  68.2 0.6 fusion.51
  68.8 0.3 fusion.52
  69.1 0.4 fusion.53
  69.4 0.6 fusion.51
  70.0 0.3 fusion.52
  70.3 0.4 fusion.53
  70.6 0.6 fusion.51
  71.2 0.3 fusion.52
  71.5 0.4 fusion.53
  71.9 0.6 fusion.51
  72.4 0.3 fusion.52
  72.7 0.4 fusion.53
  73.1 0.0 copy-done.1
  73.1 0.0 copy-start.2
  73.1 1.7 %convolution_convert_fusion.1 = bf16[256,2048]{1,0:T(8,128)(2,1)} fusion(bf16[256,384]{0,1:T(8,128)(2,1)S(1)} %bitcast.81, bf16[2048,384]{1,0:T(8,128)(2,1)S(1)} %bitcast.73), kind=kOutput, calls=%fused_computation.22 | convolution fusion | flops 403177472 | bytes 2818048 | tf_op jit(solution)/shard_map/dot_general | solution.py:273
  74.9 0.0 copy-start.3
  74.9 0.0 copy-start
  74.9 0.0 reduce-scatter.2.cloned.1.call-update
  74.9 0.0 copy-done.2
  74.9 0.1 copy.23
  75.0 0.1 reduce-window.9
  75.1 0.1 reduce.1
  75.2 0.7 gather_fusion.1
  75.9 0.7 gather_fusion
  76.6 1.3 dynamic-slice.1
  78.5 0.0 copy-done.3
  78.5 0.2 convert_reduce_fusion
  78.8 30.0 %reduce-scatter.2.cloned.1.call-done = bf16[256,512]{1,0:T(8,128)(2,1)} async-done(((bf16[256,2048]{1,0:T(8,128)(2,1)}), bf16[256,512]{1,0:T(8,128)(2,1)}) %reduce-scatter.2.cloned.1.call-update) | async-done | bytes 262160 | tf_op jit(solution)/shard_map/reduce_scatter | solution.py:297
  108.8 0.0 copy-done
  108.8 1.1 convolution_convert_fusion.2
  109.9 24.1 %all-reduce = bf16[32,512]{1,0:T(8,128)(2,1)S(1)} all-reduce(bf16[32,512]{1,0:T(8,128)(2,1)S(1)} %convolution_convert_fusion.2), channel_id=3, replica_groups=mesh['dp'=16,'seq'=8,'index'=4] {'seq'}, use_global_device_ids=true, to_apply=%region_7.8.clone | all-reduce | flops 16384 | bytes 65536
  134.0 0.7 fusion.27
  134.7 3.3 %all-to-all-start = ((f32[4,2,512]{2,1,0:T(2,128)}), f32[4,2,512]{2,1,0:T(2,128)S(1)}, u32[]{:S(2)}, u32[]{:S(2)}) async-start(f32[4,2,512]{2,1,0:T(2,128)} %fusion.27), calls=%async_computation.1 | async-start | bytes 32768 | tf_op jit(solution)/shard_map/all_to_all | solution.py:312
  138.0 1.7 %fusion.19 = bf16[1,256,512]{2,1,0:T(8,128)(2,1)} fusion(bf16[256,512]{1,0:T(8,128)(2,1)} %reduce-scatter.2.cloned.1.call-done, bf16[1,256,2048]{2,1,0:T(8,128)(2,1)S(1)} %copy-done, s32[]{:T(128)S(6)} %select_n.81), kind=kLoop, calls=%fused_computation.31 | loop fusion | flops 524288 | bytes 786436 | tf_op jit(solution)/shard_map/broadcast_in_dim | solution.py:314
  139.7 3.6 %all-to-all-done = f32[4,2,512]{2,1,0:T(2,128)S(1)} async-done(((f32[4,2,512]{2,1,0:T(2,128)}), f32[4,2,512]{2,1,0:T(2,128)S(1)}, u32[]{:S(2)}, u32[]{:S(2)}) %all-to-all-start) | async-done | bytes 16416 | tf_op jit(solution)/shard_map/all_to_all | solution.py:312
  143.3 0.1 fusion.23
  143.4 0.7 broadcast_multiply_fusion
  (12 shorter events, 0.1 us)
Async XLA Ops:
  7.2 101.6 %reduce-scatter.2.cloned.1.call-start = ((), (), s32[]{:S(2)}) async-start(), calls=%async_computation.2 | async-start | bytes 1310720 | tf_op jit(solution)/shard_map/reduce_scatter | solution.py:297
  57.5 5.3 %collective-permute-start = (bf16[2,256,384]{2,1,0:T(8,128)(2,1)S(1)}, bf16[2,256,384]{2,1,0:T(8,128)(2,1)S(1)}, u32[]{:S(2)}, u32[]{:S(2)}) collective-permute-start(bf16[2,256,384]{2,1,0:T(8,128)(2,1)S(1)} %pad_maximum_fusion.1), channel_id=1, source_target_pairs={{0,4},{4,8},{8,12},{12,16},{16,20},{20,24},{24,28},{1,5},{5,9},{9,... | collective-permute-start | bytes 1179656 | tf_op jit(solution)/shard_map/ppermute | solution.py:218
  60.4 3.6 %collective-permute-start.1 = (bf16[2,256,384]{2,1,0:T(8,128)(2,1)S(1)}, bf16[2,256,384]{2,1,0:T(8,128)(2,1)S(1)}, u32[]{:S(2)}, u32[]{:S(2)}) collective-permute-start(bf16[2,256,384]{2,1,0:T(8,128)(2,1)S(1)} %pad_maximum_fusion.1), channel_id=1, source_target_pairs={{4,0},{8,4},{12,8},{16,12},{20,16},{24,20},{28,24},{5,1},{9,5},{13... | collective-permute-start | bytes 1179656 | tf_op jit(solution)/shard_map/ppermute | solution.py:220
  65.8 7.3 %copy-start.1 = (bf16[16,128,384]{2,1,0:T(8,128)(2,1)S(1)}, bf16[16,128,384]{2,1,0:T(8,128)(2,1)}, u32[]{:S(2)}) copy-start(bf16[16,128,384]{2,1,0:T(8,128)(2,1)} %get-tuple-element.42) | copy-start | bytes 4718596
  73.1 1.8 %copy-start.2 = (s32[1,32]{1,0:T(1,128)S(1)}, s32[1,32]{1,0:T(1,128)}, u32[]{:S(2)}) copy-start(s32[1,32]{1,0:T(1,128)} %param.8) | copy-start | bytes 388
  74.9 3.7 %copy-start.3 = (s32[1,4,1]{1,2,0:T(1,128)S(1)}, s32[1,4,1]{1,2,0:T(1,128)}, u32[]{:S(2)}) copy-start(s32[1,4,1]{1,2,0:T(1,128)} %param.9) | copy-start | bytes 52
  74.9 33.9 %copy-start = (bf16[1,256,2048]{2,1,0:T(8,128)(2,1)S(1)}, bf16[1,256,2048]{2,1,0:T(8,128)(2,1)}, u32[]{:S(2)}) copy-start(bf16[1,256,2048]{2,1,0:T(8,128)(2,1)} %param.6) | copy-start | bytes 3145732
  134.7 8.6 %all-to-all-start = ((f32[4,2,512]{2,1,0:T(2,128)}), f32[4,2,512]{2,1,0:T(2,128)S(1)}, u32[]{:S(2)}, u32[]{:S(2)}) async-start(f32[4,2,512]{2,1,0:T(2,128)} %fusion.27), calls=%async_computation.1 | async-start | bytes 32768 | tf_op jit(solution)/shard_map/all_to_all | solution.py:312
Sparse Core Ops, SparseCore 0:
  75.0 33.7 reduce-scatter.1

commit v2 on v1

--- a/solution.py
+++ b/solution.py
@@ -23,7 +23,7 @@
     return jnp.cos(angles), jnp.sin(angles) * sign[None, :]
 
 
-def gather_kernel(x_ref, w_ref, cos_ref, sin_ref, q_ref, k_ref, v_ref, o_ref,
+def gather_kernel(x_ref, w_ref, cos_ref, sin_ref, q_ref, kv_ref, o_ref,
                   w_all, acc, local_sem, zs, zr, xs, xr, ps, pr):
     nz = lax.axis_size("dp")
     ns = lax.axis_size("seq")
@@ -155,12 +155,12 @@
     width = q_ref.shape[1]
     lane = lax.broadcasted_iota(jnp.int32, (q_ref.shape[0], 128), 1)
     lower = lax.rem(lane, HD) < HD // 2
-    for j, ref in ((0, q_ref), (1, k_ref)):
+    for j, ref, scale in ((0, q_ref, HD ** -0.5), (1, kv_ref.at[0], 1.0)):
         for start in range(0, width, 128):
             value = acc[j, :, start:start + 128]
             swapped = jnp.where(lower, pltpu.roll(value, 128 - HD // 2, 1), pltpu.roll(value, HD // 2, 1))
-            ref[:, start:start + 128] = (value * cos_ref[...] + swapped * sin_ref[...]).astype(jnp.bfloat16)
-    v_ref[...] = acc[2].astype(jnp.bfloat16)
+            ref[:, start:start + 128] = ((value * cos_ref[...] + swapped * sin_ref[...]) * scale).astype(jnp.bfloat16)
+    kv_ref[1] = acc[2].astype(jnp.bfloat16)
     o_ref[...] = w_all[:, 3]
 
     def finish(k, carry):
@@ -193,9 +193,9 @@
     dma = pltpu.SemaphoreType.DMA
     return pl.pallas_call(
         gather_kernel,
-        out_shape=(out, out, out, jax.ShapeDtypeStruct((nz, rows, width), jnp.bfloat16)),
+        out_shape=(out, jax.ShapeDtypeStruct((2, tokens, width), jnp.bfloat16), jax.ShapeDtypeStruct((nz, rows, width), jnp.bfloat16)),
         in_specs=[pl.BlockSpec(memory_space=VMEM)] * 4,
-        out_specs=[pl.BlockSpec(memory_space=VMEM)] * 4,
+        out_specs=[pl.BlockSpec(memory_space=VMEM)] * 3,
         scratch_shapes=[
             VMEM((nz, pieces, rows, width), jnp.bfloat16),
             VMEM((3, tokens, width), jnp.float32),
@@ -207,111 +207,242 @@
     )(states, weights, cosine, sine)
 
 
-def with_halo(cells, sides, width):
-    for axis, dim in sides:
-        count = lax.axis_size(axis)
-        ends = count - 1
-        head = lax.slice_in_dim(cells, 0, width, axis=dim)
-        tail = lax.slice_in_dim(cells, cells.shape[dim] - width, cells.shape[dim], axis=dim)
-        cells = jnp.concatenate(
-            [
-                lax.ppermute(tail, axis, [(i, (i + 1) % count) for i in range(ends)]),
-                cells,
-                lax.ppermute(head, axis, [((i + 1) % count, i) for i in range(ends)]),
-            ],
-            axis=dim,
-        )
-    return cells
-
-
-def window_heads(queries, key_rows, value_rows, visible):
-    scale = HD ** (-0.5)
-
-    def one_head(items):
-        query_head, key_head, value_head = items
-        scores = jnp.dot(query_head, key_head.T, preferred_element_type=jnp.float32) * scale
-        scores = jnp.where(visible, scores, -1e30)
-        maxima = jnp.max(scores, -1, keepdims=True)
-        expo = jnp.exp(scores - maxima)
-        weights = (expo / jnp.sum(expo, -1, keepdims=True)).astype(jnp.bfloat16)
-        return jnp.dot(weights, value_head, preferred_element_type=jnp.float32).astype(jnp.bfloat16)
-
-    context = lax.map(
-        one_head,
-        (jnp.moveaxis(queries, 1, 0), jnp.moveaxis(key_rows, 1, 0), jnp.moveaxis(value_rows, 1, 0)),
-    )
-    return jnp.moveaxis(context, 0, 1)
+def attend_kernel(shard_ref, len_ref, x_ref, q_ref, kv_ref, o_ref, layer_ref, shelf_ref,
+                  side, ctx, w3, layer_buf, send_pool, pools, route, shelves,
+                  hs, hr, cs, cr, ws, wr, ps, pr, ls, ss, sr, rs, rr):
+    ns = lax.axis_size("seq")
+    ny = lax.axis_size("index")
+    s = lax.axis_index("seq")
+    y = lax.axis_index("index")
+    core = lax.rem(s, 2)
+    partner = s + 1 - 2 * core
+    tokens, width = q_ref.shape
+    pairs = width // 128
+    quarter = layer_ref.shape[1]
+
+    def remote(src, dst, send, recv, device):
+        return pltpu.make_async_remote_copy(src_ref=src, dst_ref=dst, send_sem=send, recv_sem=recv,
+                                            device_id=device, device_id_type=MESH)
+
+    barrier = pltpu.get_barrier_semaphore()
+    for k in range(1, ns):
+        pl.semaphore_signal(barrier, inc=1, device_id={"seq": lax.rem(s + k, ns)}, device_id_type=MESH)
+    for k in range(1, ny):
+        pl.semaphore_signal(barrier, inc=1, device_id={"index": lax.rem(y + k, ny)}, device_id_type=MESH)
+    pl.semaphore_wait(barrier, ns + ny - 2)
+
+    after = {"seq": lax.rem(s + 1, ns)}
+    before = {"seq": lax.rem(s + ns - 1, ns)}
+
+    def halo_copy(which, pair):
+        ref = kv_ref.at[:, :, pl.ds(pair * 128, 128)]
+        return remote(ref, side.at[which, pair], hs.at[which, pair], hr.at[which, pair], (after, before)[which])
+
+    for pair in range(pairs):
+        for which in range(2):
+            halo_copy(which, pair).start()
+
+    owned = o_ref.shape[0] // ny
+
+    def w_copy(k):
+        t = lax.rem(y + k, ny)
+        src = o_ref.at[pl.ds(t * owned + 2 * core, 2)]
+        return remote(src, w3.at[y, pl.ds(2 * core, 2)], ws.at[k], wr.at[y], {"index": t})
+
+    def w_wait(k):
+        f = lax.rem(y + k, ny)
+        ref = w3.at[f, pl.ds(2 * core, 2)]
+        remote(ref, ref, ws.at[k], wr.at[f], {"index": f}).wait_recv()
+
+    def mate_copy(k):
+        f = lax.rem(y + k, ny)
+        ref = w3.at[f, pl.ds(2 * core, 2)]
+        return remote(ref, ref, ps.at[f], pr.at[f], {"seq": partner})
+
+    def mate_wait(k):
+        f = lax.rem(y + k, ny)
+        ref = w3.at[f, pl.ds(2 - 2 * core, 2)]
+        remote(ref, ref, ps.at[f], pr.at[f], {"seq": partner}).wait_recv()
+
+    for k in (1, 3, 2):
+        w_copy(k).start()
+    own = pltpu.make_async_copy(o_ref.at[pl.ds(y * owned, owned)], w3.at[y], ls)
+    own.start()
+
+    row = lax.broadcasted_iota(jnp.int32, (tokens, tokens), 0)
+    col = lax.broadcasted_iota(jnp.int32, (tokens, tokens), 1)
+    see_before = jnp.logical_and(col >= row, s > 0)
+    see_after = jnp.logical_and(col <= row, s < ns - 1)
+    lane = lax.broadcasted_iota(jnp.int32, (tokens, 128), 1)
+
+    def ctx_copy(pair, k):
+        t = lax.rem(y + k, ny)
+        ref = ctx.at[y, pair]
+        return remote(ref, ref, cs.at[pair, k], cr.at[pair, y], {"index": t})
+
+    def ctx_wait(pair, k):
+        f = lax.rem(y + k, ny)
+        ref = ctx.at[f, pair]
+        remote(ref, ref, cs.at[pair, k], cr.at[pair, f], {"index": f}).wait_recv()
+
+    def scores(query, key):
+        return lax.dot_general(query, key, (((1,), (1,)), ((), ())), preferred_element_type=jnp.float32)
+
+    for pair in range(pairs):
+        cols = pl.ds(pair * 128, 128)
+        query = q_ref[:, cols]
+        for which in range(2):
+            halo_copy(which, pair).wait_recv()
+        results = []
+        for head in range(2):
+            inside = (lane < HD) if head == 0 else (lane >= HD)
+            chosen = jnp.where(inside, query, jnp.zeros_like(query))
+            low = jnp.where(see_before, scores(chosen, side[0, pair, 0]), -1e30)
+            mid = scores(chosen, kv_ref[0, :, cols])
+            high = jnp.where(see_after, scores(chosen, side[1, pair, 0]), -1e30)
+            top = jnp.max(jnp.maximum(jnp.maximum(low, mid), high), axis=1, keepdims=True)
+            low, mid, high = jnp.exp(low - top), jnp.exp(mid - top), jnp.exp(high - top)
+            total = jnp.sum(low + mid + high, axis=1, keepdims=True)
+            value = jnp.dot(low.astype(jnp.bfloat16), side[0, pair, 1], preferred_element_type=jnp.float32)
+            value += jnp.dot(mid.astype(jnp.bfloat16), kv_ref[1, :, cols], preferred_element_type=jnp.float32)
+            value += jnp.dot(high.astype(jnp.bfloat16), side[1, pair, 1], preferred_element_type=jnp.float32)
+            results.append(value / total)
+        ctx[y, pair] = jnp.where(lane < HD, results[0], results[1]).astype(jnp.bfloat16)
+        for k in (1, 3, 2):
+            ctx_copy(pair, k).start()
+        w_wait((1, 3, 2)[pair])
+        mate_copy((1, 3, 2)[pair]).start()
+
+    def project(k):
+        f = lax.rem(y + k, ny)
+        context = jnp.concatenate([ctx[f, pair] for pair in range(pairs)], axis=1)
+        return jnp.concatenate([scores(context, w3[f, part]) for part in range(owned)], axis=1)
+
+    own.wait()
+    summed = x_ref[:, pl.ds(pl.multiple_of(y * quarter, 128), quarter)].astype(jnp.float32) + project(0)
+    for k in (1, 3, 2):
+        mate_wait(k)
+        for pair in range(pairs):
+            ctx_wait(pair, k)
+        summed += project(k)
+    layer = summed.astype(jnp.bfloat16)
+    layer_ref[...] = layer
+
+    count = len_ref.shape[1]
+    per_block = count // ns
+    slots = ns * 8
+    slot = lax.broadcasted_iota(jnp.int32, (slots, count), 0)
+    stretch = lax.rem(slot, 8) * ns + slot // 8
+    which_stretch = lax.broadcasted_iota(jnp.int32, (slots, count), 1)
+    lengths = jnp.broadcast_to(len_ref[...], (slots, count))
+    ends = jnp.sum(jnp.where(which_stretch <= stretch, lengths, 0), axis=1, keepdims=True)
+    starts = jnp.sum(jnp.where(which_stretch < stretch, lengths, 0), axis=1, keepdims=True)
+    position = lax.broadcasted_iota(jnp.int32, (slots, tokens), 1) + s * tokens
+    real = lax.rem(lax.broadcasted_iota(jnp.int32, (slots, tokens), 0), 8) < per_block
+    inside = jnp.logical_and(jnp.logical_and(position >= starts, position < ends), real)
+    member = jnp.where(inside, 1.0, 0.0).astype(jnp.bfloat16)
+    partial = jnp.dot(member, layer, preferred_element_type=jnp.float32)
+    send_pool[...] = partial.reshape(ns, 8, quarter)
+
+    def pool_copy(k):
+        t = lax.rem(s + k, ns)
+        return remote(send_pool.at[t], pools.at[s], ss.at[k], sr.at[s], {"seq": t})
+
+    def pool_wait(k):
+        f = lax.rem(s + k, ns)
+        remote(send_pool.at[f], pools.at[f], ss.at[k], sr.at[f], {"seq": f}).wait_recv()
+
+    for k in range(1, ns):
+        pool_copy(k).start()
+    pooled = send_pool[s]
+    for k in range(1, ns):
+        pool_wait(k)
+    for k in range(1, ns):
+        pooled += pools[lax.rem(s + k, ns)]
+
+    ids = [shard_ref[i] for i in range(per_block)]
+    line = lax.broadcasted_iota(jnp.int32, (8, quarter), 0)
+    places = []
+    for i in range(per_block):
+        rank = jnp.int32(0)
+        for j in range(i):
+            rank += jnp.where(ids[j] == ids[i], 1, 0)
+        places.append(ids[i] * (per_block // 2) + rank)
+    rows = [jnp.broadcast_to(pooled[i:i + 1], (8, quarter)) for i in range(per_block)]
+    for r in range(ny):
+        held = jnp.zeros((8, quarter), jnp.float32)
+        for i in range(per_block):
+            held += jnp.where(line == places[i] - r * (per_block // 2), rows[i], 0.0)
+        route[r] = held
+
+    def route_copy(k):
+        t = lax.rem(y + k, ny)
+        return remote(route.at[t], shelves.at[y], rs.at[k], rr.at[y], {"index": t})
+
+    def route_wait(k):
+        f = lax.rem(y + k, ny)
+        remote(route.at[f], shelves.at[f], rs.at[k], rr.at[f], {"index": f}).wait_recv()
+
+    for k in range(1, ny):
+        route_copy(k).start()
+    shelves[y] = route[y]
+    for k in range(1, ny):
+        route_wait(k)
+    found = jnp.concatenate([shelves[f, 0:per_block // 2] for f in range(ny)], axis=1)
+    mean = jnp.sum(found * found, axis=1, keepdims=True) / (quarter * ny)
+    shelf_ref[...] = found * lax.rsqrt(mean + 1e-6)
+
+    for pair in range(pairs):
+        for which in range(2):
+            halo_copy(which, pair).wait_send()
+        for k in range(1, ny):
+            ctx_copy(pair, k).wait_send()
+    for k in range(1, ny):
+        w_copy(k).wait_send()
+        mate_copy(k).wait_send()
+        route_copy(k).wait_send()
+    for k in range(1, ns):
+        pool_copy(k).wait_send()
+
+
+def attended(shards, lengths, states, queries, pair_kv, out_rows):
+    tokens, width = queries.shape
+    ny = lax.axis_size("index")
+    ns = lax.axis_size("seq")
+    nz, rows, _ = out_rows.shape
+    pairs = width // 128
+    quarter = nz * rows // ny
+    slots = shards.shape[0] // 2
+    dma = pltpu.SemaphoreType.DMA
+    return pl.pallas_call(
+        attend_kernel,
+        out_shape=(jax.ShapeDtypeStruct((tokens, quarter), jnp.bfloat16),
+                   jax.ShapeDtypeStruct((slots, quarter * ny), jnp.float32)),
+        in_specs=[pl.BlockSpec(memory_space=pltpu.SMEM)] + [pl.BlockSpec(memory_space=VMEM)] * 5,
+        out_specs=[pl.BlockSpec(memory_space=VMEM)] * 2,
+        scratch_shapes=[
+            VMEM((2, pairs, 2, tokens, 128), jnp.bfloat16),
+            VMEM((ny, pairs, tokens, 128), jnp.bfloat16),
+            VMEM((ny, nz // ny, rows, width), jnp.bfloat16),
+            VMEM((8, 128), jnp.float32),
+            VMEM((ns, 8, quarter), jnp.float32), VMEM((ns, 8, quarter), jnp.float32),
+            VMEM((ny, 8, quarter), jnp.float32), VMEM((ny, 8, quarter), jnp.float32),
+            dma((2, pairs)), dma((2, pairs)), dma((pairs, ny)), dma((pairs, ny)),
+            dma((ny,)), dma((ny,)), dma((ny,)), dma((ny,)), dma(()),
+            dma((ns,)), dma((ns,)), dma((ny,)), dma((ny,)),
+        ],
+        compiler_params=pltpu.CompilerParams(collective_id=1, has_side_effects=True),
+    )(shards, lengths, states, queries, pair_kv, out_rows)
 
 
 def body(hidden, proj_weight, stretch_lengths, shard_of):
     states = hidden[0]
     tokens_here = states.shape[0]
-    width = proj_weight.shape[2]
-    heads_here = width // HD
-    seq_index = lax.axis_index("seq")
-    group_index = lax.axis_index("index")
-    seq_count = lax.axis_size("seq")
-    index_count = lax.axis_size("index")
-    total_length = tokens_here * seq_count
-    positions = seq_index * tokens_here + jnp.arange(tokens_here, dtype=jnp.int32)
+    positions = lax.axis_index("seq") * tokens_here + jnp.arange(tokens_here, dtype=jnp.int32)
     cosine, sine = rope_tables(positions, 128)
-    queries, keys, value_rows, out_rows = gathered_projection(states, proj_weight, cosine, sine)
-    out_rows_full = out_rows.reshape(-1, width)
-    queries = queries.reshape(tokens_here, heads_here, HD)
-    stacked = jnp.stack([keys, value_rows])
-    padded = with_halo(stacked, (("seq", 1),), HALF_WIN)
-    span = tokens_here + 2 * HALF_WIN
-    key_part = padded[0, 0:span].reshape(span, heads_here, HD)
-    value_part = padded[1, 0:span].reshape(span, heads_here, HD)
-    key_pos = seq_index * tokens_here + 0 - HALF_WIN + jnp.arange(span, dtype=jnp.int32)
-    visible = (
-        (jnp.abs(key_pos[None, :] - positions[:, None]) <= HALF_WIN)
-        & (key_pos[None, :] >= 0)
-        & (key_pos[None, :] < total_length)
-    )
-    context_parts = window_heads(queries, key_part, value_part, visible).reshape(tokens_here, width)
-    partial_value = lax.dot_general(
-        context_parts, out_rows_full, (((1,), (1,)), ((), ())), preferred_element_type=jnp.float32
-    )
-    lengths = stretch_lengths[0]
-    stretch_count = lengths.shape[0]
-    per_block = stretch_count // seq_count
-    ends = jnp.cumsum(lengths, dtype=jnp.int32)
-    starts = ends - lengths
-    row_ids = jnp.arange(stretch_count, dtype=jnp.int32)
-    order = row_ids % per_block * seq_count + row_ids // per_block
-    row_starts = starts[order]
-    row_ends = ends[order]
-    member = (
-        (positions[None, :] >= row_starts[:, None]) & (positions[None, :] < row_ends[:, None])
-    ).astype(jnp.bfloat16)
-    shard_ids = shard_of[0, :, 0]
-    local_rows = jnp.arange(per_block, dtype=jnp.int32)
-    earlier = (shard_ids[:, None] == shard_ids[None, :]) & (
-        local_rows[None, :] < local_rows[:, None]
-    )
-    slot_rank = jnp.sum(earlier.astype(jnp.int32), 1)
-    capacity = per_block // 2
-    slot_ids = jnp.arange(capacity, dtype=jnp.int32)
-    quarter = D // index_count
-    summed = lax.psum_scatter(
-        partial_value.astype(jnp.bfloat16), "index", scatter_dimension=1, tiled=True
-    ).astype(jnp.float32)
-    own_states = lax.dynamic_slice_in_dim(states, group_index * quarter, quarter, 1)
-    layer = (own_states.astype(jnp.float32) + summed).astype(jnp.bfloat16)
-    partial_pool = jnp.dot(member, layer, preferred_element_type=jnp.float32)
-    pooled = lax.psum_scatter(
-        partial_pool.astype(jnp.bfloat16), "seq", scatter_dimension=0, tiled=True
-    ).astype(jnp.float32)
-    shard_range = jnp.arange(index_count, dtype=jnp.int32)
-    routing = (
-        (shard_ids[None, None, :] == shard_range[:, None, None])
-        & (slot_rank[None, None, :] == slot_ids[None, :, None])
-    ).astype(jnp.float32)
-    outgoing = jnp.einsum("rkc,cf->rkf", routing, pooled, precision=lax.Precision.HIGHEST)
-    arrived = lax.all_to_all(outgoing, "index", split_axis=0, concat_axis=2, tiled=True)[0]
-    shelf_rows = arrived * lax.rsqrt(jnp.mean(arrived * arrived, -1, keepdims=True) + 1e-06)
-    return (layer[None], shelf_rows[None, None, None])
+    queries, pair_kv, out_rows = gathered_projection(states, proj_weight, cosine, sine)
+    layer, shelf = attended(shard_of[0, :, 0], stretch_lengths, states, queries, pair_kv, out_rows)
+    return (layer[None], shelf[None, None, None])
 
 
 def solution(mesh):

time: 151 us -> 90.5 us (0.60)
  the two profiles are of different devices: /device:TPU:32 before, /device:TPU:1 now
where the time goes in v2:
time: 90.5 us; the launch traced here: 90.2 us
  Pallas kernels  85.3 us (94%)
  local copies, waits for them, and re-layouts  2.99 us (3%)
  other arithmetic  1.26 us (1%)
    pallas_call x1, Pallas kernels, gathered_projection(): pl.pallas_call(gather_kernel, out_shape=(out, jax.ShapeDtypeStruct((2, to...  51.4 us
    pallas_call x1, Pallas kernels, attended(): pl.pallas_call(attend_kernel, out_shape=(jax.ShapeDtypeStruct((tokens, qu...  33.9 us
    unnamed x2, local copies, waits for them, and re-layouts  2.99 us

profile of v2, /device:TPU:1, one launch (start us, length us, event | category | flops | bytes accessed | tf_op | source)
XLA Modules:
  0.0 90.2 jit_solution(143107180817194360)
XLA Ops:
  0.7 1.2 %fusion = (f32[256,128]{1,0:T(8,128)}, f32[256,128]{1,0:T(8,128)}) fusion(f32[128]{0:T(128)S(1)} %get-tuple-element.14, f32[128]{0:T(128)S(1)} %get-tuple-element.15, f32[256]{0:T(256)S(1)} %add_convert_fusion), kind=kLoop, calls=%fused_computation.2 | loop fusion | flops 65536 | bytes 264192 | tf_op jit(solution)/shard_map/mul | solution.py:23
  1.9 51.4 %shard_map.59 = (bf16[256,384]{1,0:T(8,128)(2,1)}, bf16[2,256,384]{2,1,0:T(8,128)(2,1)}, bf16[16,128,384]{2,1,0:T(8,128)(2,1)}) custom-call(bf16[256,2048]{1,0:T(8,128)(2,1)} %bitcast.4, bf16[4,128,384]{2,1,0:T(8,128)(2,1)} %w_ref.1, f32[256,128]{1,0:T(8,128)} %get-tuple-element.13.cos_ref, f32[256,128]{1,0:T(8,128)} %get-tuple-element.12.sin_ref), custom_call_target="tpu_custom_call" | custom-call | tf_op jit(solution)/shard_map/pallas_call | solution.py:194
  53.3 33.9 %shard_map.60 = (bf16[256,512]{1,0:T(8,128)(2,1)}, f32[2,2048]{1,0:T(2,128)}) custom-call(s32[4]{0:T(128)} %bitcast.8, s32[1,32]{1,0:T(1,128)} %len_ref.1, bf16[256,2048]{1,0:T(8,128)(2,1)} %bitcast.5, bf16[256,384]{1,0:T(8,128)(2,1)} %get-tuple-element.7.q_ref, bf16[2,256,384]{2,1,0:T(8,128)(2,1)} %get-tuple-element.8.kv_ref, ...), custom_call_target="tpu_custom_call" | custom-call | tf_op jit(solution)/shard_map/pallas_call | solution.py:417
  87.2 1.7 %copy.8 = bf16[1,256,512]{2,1,0:T(8,128)(2,1)} copy(bf16[1,256,512]{2,1,0:T(8,128)(2,1)} %bitcast.6) | data formatting | bytes 524288
  88.9 1.3 %copy.9 = f32[1,1,1,2,2048]{4,3,2,1,0:T(2,128)} copy(f32[1,1,1,2,2048]{4,3,2,1,0:T(2,128)} %bitcast.7) | data formatting | bytes 32768
  (2 shorter events, 0.0 us)

commit v3 on v0

v3 whole, which is shorter than its diff:
```python
import jax
import jax.numpy as jnp
from jax import lax
from jax.experimental import pallas as pl
from jax.experimental.pallas import tpu as pltpu
from jax.sharding import PartitionSpec as P

HD = 64
MESH = pl.DeviceIdType.MESH
VMEM = pltpu.VMEM


def layer_kernel(shard_ref, len_ref, x_hbm, w_hbm, layer_ref, shelf_ref,
                 x_ref, w_all, w3_ring, w3, acc, queries, pair_kv, side, ctx, send_pool, pools, route, shelves,
                 local, zs, zr, xs, xr, ps, pr, ys, yr, yl, ws, wr, ms, mr,
                 hs, hr, cs, cr, fs, fr, ss, sr, rs, rr):
    nz = lax.axis_size("dp")
    ns = lax.axis_size("seq")
    ny = lax.axis_size("index")
    z = lax.axis_index("dp")
    s = lax.axis_index("seq")
    y = lax.axis_index("index")
    pieces, rows, width = w_hbm.shape
    tokens = x_ref.shape[0]
    pairs = width // 128
    quarter = layer_ref.shape[1]
    owned = nz // ny
    core = lax.rem(s, 2)
    par = lax.rem(s // 2, 2)
    mate = {"seq": s + 1 - 2 * core}
    right = {"seq": lax.rem(s + 2, ns)}
    left = {"seq": lax.rem(s + ns - 2, ns)}
    after = {"seq": lax.rem(s + 1, ns)}
    before = {"seq": lax.rem(s + ns - 1, ns)}

    def remote(src, dst, send, recv, device):
        return pltpu.make_async_remote_copy(src_ref=src, dst_ref=dst, send_sem=send, recv_sem=recv,
                                            device_id=device, device_id_type=MESH)

    def shifted(d):
        return lax.rem(z + nz + d, nz)

    x_load = pltpu.make_async_copy(x_hbm, x_ref, local.at[0])
    x_load.start()
    own_load = pltpu.make_async_copy(w_hbm.at[pl.ds(0, 3)], w_all.at[z], local.at[1])
    own_load.start()

    barrier = pltpu.get_barrier_semaphore()
    for d in (1, -1):
        pl.semaphore_signal(barrier, inc=1, device_id={"dp": shifted(d)}, device_id_type=MESH)
    for k in range(1, ns):
        pl.semaphore_signal(barrier, inc=1, device_id={"seq": lax.rem(s + k, ns)}, device_id_type=MESH)
    for k in range(1, ny):
        pl.semaphore_signal(barrier, inc=1, device_id={"index": lax.rem(y + k, ny)}, device_id_type=MESH)
    pl.semaphore_wait(barrier, ns + ny)

    part = rows // 4
    sub = part // 2
    mine = pl.multiple_of(rows // 2 * par + part * core, 16)
    other = pl.multiple_of(rows // 2 * (1 - par) + part * core, 16)
    mate_mine = pl.multiple_of(rows // 2 * par + part * (1 - core), 16)
    mate_other = pl.multiple_of(rows // 2 * (1 - par) + part * (1 - core), 16)

    far = nz // 2
    edges = {}
    for d in range(far):
        for sign in ((1, -1) if d < far - 1 else (1,)):
            edges[sign * d, sign * (d + 1)] = len(edges)

    def z_ref(g, o):
        return w3_ring.at[o] if g == 3 else w_all.at[o, g, pl.ds(mine, part)]

    def z_copy(g, here, there):
        o = shifted(-here)
        dst = z_ref(g, o)
        src = w_hbm.at[g, pl.ds(mine, part)] if here == 0 else dst
        return remote(src, dst, zs.at[g, edges[here, there]], zr.at[g, o], {"dp": shifted(there - here)})

    def z_wait(g, d):
        o = shifted(-d)
        remote(z_ref(g, o), z_ref(g, o), zs.at[g, 0], zr.at[g, o], {"dp": shifted(1)}).wait_recv()

    def forward(g, d):
        for here, there in edges:
            if here == d:
                z_copy(g, here, there).start()

    def x_copy(o, which):
        ref = w_all.at[o, :, pl.ds(mine + which * sub, sub)]
        return remote(ref, ref, xs.at[which, o], xr.at[which, o], (right, left)[which])

    def x_wait(o, which):
        ref = w_all.at[o, :, pl.ds(other + which * sub, sub)]
        remote(ref, ref, xs.at[which, o], xr.at[which, o], right).wait_recv()

    def p_copy(o, which):
        ref = w_all.at[o, :, pl.ds((mine, other)[which], part)]
        return remote(ref, ref, ps.at[which, o], pr.at[which, o], mate)

    def p_wait(o, which):
        ref = w_all.at[o, :, pl.ds((mate_mine, mate_other)[which], part)]
        remote(ref, ref, ps.at[which, o], pr.at[which, o], mate).wait_recv()

    def y_local(d):
        o = shifted(-d)
        src = w_hbm.at[3, pl.ds(mine, part)] if d == 0 else w3_ring.at[o]
        j = lax.rem(o, owned)
        return pltpu.make_async_copy(src, w3.at[y, j, pl.ds(mine, part)], yl.at[j])

    def y_copy(d):
        o = shifted(-d)
        src = w_hbm.at[3, pl.ds(mine, part)] if d == 0 else w3_ring.at[o]
        j = lax.rem(o, owned)
        return remote(src, w3.at[y, j, pl.ds(mine, part)], ys.at[o], yr.at[y, j], {"index": o // owned})

    def y_start(d):
        stays = shifted(-d) // owned == y

        @pl.when(stays)
        def _():
            y_local(d).start()

        @pl.when(jnp.logical_not(stays))
        def _():
            y_copy(d).start()

    def y_finish(d):
        @pl.when(shifted(-d) // owned != y)
        def _():
            y_copy(d).wait_send()

    def w_copy(j, which):
        ref = w3.at[:, j, pl.ds(mine + which * sub, sub)]
        return remote(ref, ref, ws.at[which, j], wr.at[which, j], (right, left)[which])

    def w_wait(j, which):
        ref = w3.at[:, j, pl.ds(other + which * sub, sub)]
        remote(ref, ref, ws.at[which, j], wr.at[which, j], right).wait_recv()

    def m_copy(j, which):
        ref = w3.at[:, j, pl.ds((mine, other)[which], part)]
        return remote(ref, ref, ms.at[which, j], mr.at[which, j], mate)

    def m_wait(j, which):
        ref = w3.at[:, j, pl.ds((mate_mine, mate_other)[which], part)]
        remote(ref, ref, ms.at[which, j], mr.at[which, j], mate).wait_recv()

    def w_arrive(d):
        o = shifted(-d)
        j = lax.rem(o, owned)

        @pl.when(o // owned == y)
        def _():
            y_local(d).wait()
            for k in range(1, ny):
                f = lax.rem(y + k, ny)
                ref = w3.at[f, j, pl.ds(mine, part)]
                remote(ref, ref, ys.at[0], yr.at[f, j], {"index": f}).wait_recv()
            for which in range(2):
                w_copy(j, which).start()
            m_copy(j, 0).start()

    def w_cross(d):
        o = shifted(-d)
        j = lax.rem(o, owned)

        @pl.when(o // owned == y)
        def _():
            for which in range(2):
                w_wait(j, which)
            m_copy(j, 1).start()

    for g in range(pieces):
        forward(g, 0)
    y_start(0)

    half = HD // 2
    lane = lax.broadcasted_iota(jnp.int32, (tokens, 128), 1)
    lower = lax.rem(lane, HD) < half
    freqs = jnp.exp(lax.rem(lane, half).astype(jnp.float32) * (-2.0 / HD * 9.210340371976184))
    angles = (lax.broadcasted_iota(jnp.int32, (tokens, 128), 0) + s * tokens).astype(jnp.float32) * freqs
    cosine = jnp.cos(angles)
    sine = jnp.sin(angles)
    sine = jnp.where(lower, -sine, sine)

    acc[...] = jnp.zeros_like(acc)
    x_load.wait()
    own_load.wait()

    def arrive(ds):
        for d in ds:
            for g in range(3):
                z_wait(g, d)
                forward(g, d)
            for which in range(2):
                x_copy(shifted(-d), which).start()
            p_copy(shifted(-d), 0).start()
        for d in ds:
            z_wait(3, d)
            forward(3, d)
            y_start(d)

    def cross(ds):
        for d in ds:
            for which in range(2):
                x_wait(shifted(-d), which)
            p_copy(shifted(-d), 1).start()

    def settle(ds):
        for d in ds:
            for which in range(2):
                p_wait(shifted(-d), which)
        a, b = (shifted(-d) for d in (ds if len(ds) == 2 else (0, ds[0])))
        lhs = jnp.concatenate([x_ref[:, pl.ds(pl.multiple_of(o * rows, 128), rows)] for o in (a, b)], axis=1)
        for j in range(3):
            rhs = jnp.concatenate([w_all[a, j], w_all[b, j]], axis=0)
            acc[j] += jnp.dot(lhs, rhs, preferred_element_type=jnp.float32)

    order = [(d, -d) for d in range(1, far)] + [(far,)]
    for i in range(len(order) + 2):
        if i < len(order):
            arrive(order[i])
        if 1 <= i <= len(order):
            cross(order[i - 1])
            for d in order[i - 1] + ((0,) if i == 1 else ()):
                w_arrive(d)
        if i >= 2:
            settle(order[i - 2])
            for d in order[i - 2] + ((0,) if i == 2 else ()):
                w_cross(d)

    for j in (1, 0):
        for pair in range(pairs):
            cols = slice(pair * 128, pair * 128 + 128)
            value = acc[j, :, cols]
            swapped = jnp.where(lower, pltpu.roll(value, 128 - half, 1), pltpu.roll(value, half, 1))
            turned = value * cosine + swapped * sine
            if j == 0:
                queries[pair] = (turned * HD ** -0.5).astype(jnp.bfloat16)
            else:
                pair_kv[pair, 0] = turned.astype(jnp.bfloat16)
                pair_kv[pair, 1] = acc[2, :, cols].astype(jnp.bfloat16)
                for which in range(2):
                    remote(pair_kv.at[pair], side.at[which, pair], hs.at[which, pair], hr.at[which, pair],
                           (after, before)[which]).start()

    def halo(which, pair):
        return remote(pair_kv.at[pair], side.at[which, pair], hs.at[which, pair], hr.at[which, pair],
                      (after, before)[which])

    row = lax.broadcasted_iota(jnp.int32, (tokens, tokens), 0)
    col = lax.broadcasted_iota(jnp.int32, (tokens, tokens), 1)
    see_before = jnp.logical_and(col >= row, s > 0)
    see_after = jnp.logical_and(col <= row, s < ns - 1)

    def beside(k):
        return {"index": lax.rem(y + k, ny)}

    def c_copy(pair, k):
        ref = ctx.at[y, pair]
        return remote(ref, ref, cs.at[pair, k], cr.at[pair, y], beside(k))

    def c_wait(pair, k):
        f = lax.rem(y + k, ny)
        ref = ctx.at[f, pair]
        remote(ref, ref, cs.at[pair, k], cr.at[pair, f], beside(k)).wait_recv()

    def f_copy(pair, k):
        f = lax.rem(y + k, ny)
        ref = ctx.at[f, pair, pl.ds(0 if k == 3 else tokens // 2, tokens // 2)]
        return remote(ref, ref, fs.at[pair, k // 2], fr.at[pair, k // 2], beside(ny - k))

    def f_wait(pair, k):
        f = lax.rem(y + 2, ny)
        ref = ctx.at[f, pair, pl.ds(0 if k == 3 else tokens // 2, tokens // 2)]
        remote(ref, ref, fs.at[pair, k // 2], fr.at[pair, k // 2], beside(k)).wait_recv()

    def relay(pair):
        for k in (1, 3):
            c_wait(pair, k)
            f_copy(pair, k).start()

    def scores(query, key):
        return lax.dot_general(query, key, (((1,), (1,)), ((), ())), preferred_element_type=jnp.float32)

    for pair in range(pairs):
        query = queries[pair]
        for which in range(2):
            halo(which, pair).wait_recv()
        results = []
        for head in range(2):
            inside = (lane < HD) if head == 0 else (lane >= HD)
            chosen = jnp.where(inside, query, jnp.zeros_like(query))
            low = jnp.where(see_before, scores(chosen, side[0, pair, 0]), -1e30)
            mid = scores(chosen, pair_kv[pair, 0])
            high = jnp.where(see_after, scores(chosen, side[1, pair, 0]), -1e30)
            top = jnp.max(jnp.maximum(jnp.maximum(low, mid), high), axis=1, keepdims=True)
            low, mid, high = jnp.exp(low - top), jnp.exp(mid - top), jnp.exp(high - top)
            total = jnp.sum(low + mid + high, axis=1, keepdims=True)
            value = jnp.dot(low.astype(jnp.bfloat16), side[0, pair, 1], preferred_element_type=jnp.float32)
            value += jnp.dot(mid.astype(jnp.bfloat16), pair_kv[pair, 1], preferred_element_type=jnp.float32)
            value += jnp.dot(high.astype(jnp.bfloat16), side[1, pair, 1], preferred_element_type=jnp.float32)
            results.append(value / total)
        ctx[y, pair] = jnp.where(lane < HD, results[0], results[1]).astype(jnp.bfloat16)
        for k in (1, 3):
            c_copy(pair, k).start()
        if pair > 0:
            relay(pair - 1)

    def project(k):
        f = lax.rem(y + k, ny)
        context = jnp.concatenate([ctx[f, pair] for pair in range(pairs)], axis=1)
        return jnp.concatenate([scores(context, w3[f, j]) for j in range(owned)], axis=1)

    for j in range(owned):
        for which in range(2):
            m_wait(j, which)
    summed = x_ref[:, pl.ds(pl.multiple_of(y * quarter, 128), quarter)].astype(jnp.float32) + project(0)
    relay(pairs - 1)
    summed += project(1)
    summed += project(3)
    for pair in range(pairs):
        for k in (1, 3):
            f_wait(pair, k)
    summed += project(2)
    layer = summed.astype(jnp.bfloat16)
    layer_ref[...] = layer

    count = len_ref.shape[1]
    per_block = count // ns
    slots = ns * 8
    slot = lax.broadcasted_iota(jnp.int32, (slots, count), 0)
    stretch = lax.rem(slot, 8) * ns + slot // 8
    which_stretch = lax.broadcasted_iota(jnp.int32, (slots, count), 1)
    lengths = jnp.broadcast_to(len_ref[...], (slots, count))
    ends = jnp.sum(jnp.where(which_stretch <= stretch, lengths, 0), axis=1, keepdims=True)
    starts = jnp.sum(jnp.where(which_stretch < stretch, lengths, 0), axis=1, keepdims=True)
    position = lax.broadcasted_iota(jnp.int32, (slots, tokens), 1) + s * tokens
    real = lax.rem(lax.broadcasted_iota(jnp.int32, (slots, tokens), 0), 8) < per_block
    inside = jnp.logical_and(jnp.logical_and(position >= starts, position < ends), real)
    member = jnp.where(inside, 1.0, 0.0).astype(jnp.bfloat16)
    partial = jnp.dot(member, layer, preferred_element_type=jnp.float32)
    send_pool[...] = partial.reshape(ns, 8, quarter)

    def pool_copy(k):
        t = lax.rem(s + k, ns)
        return remote(send_pool.at[t], pools.at[s], ss.at[k], sr.at[s], {"seq": t})

    def pool_wait(k):
        f = lax.rem(s + k, ns)
        remote(send_pool.at[f], pools.at[f], ss.at[k], sr.at[f], {"seq": f}).wait_recv()

    for k in range(1, ns):
        pool_copy(k).start()
    pooled = send_pool[s]
    for k in range(1, ns):
        pool_wait(k)
    for k in range(1, ns):
        pooled += pools[lax.rem(s + k, ns)]

    ids = [shard_ref[i] for i in range(per_block)]
    line = lax.broadcasted_iota(jnp.int32, (8, quarter), 0)
    places = []
    for i in range(per_block):
        rank = jnp.int32(0)
        for j in range(i):
            rank += jnp.where(ids[j] == ids[i], 1, 0)
        places.append(ids[i] * (per_block // 2) + rank)
    lines = [jnp.broadcast_to(pooled[i:i + 1], (8, quarter)) for i in range(per_block)]
    for r in range(ny):
        held = jnp.zeros((8, quarter), jnp.float32)
        for i in range(per_block):
            held += jnp.where(line == places[i] - r * (per_block // 2), lines[i], 0.0)
        route[r] = held

    def route_copy(k):
        t = lax.rem(y + k, ny)
        return remote(route.at[t], shelves.at[y], rs.at[k], rr.at[y], {"index": t})

    def route_wait(k):
        f = lax.rem(y + k, ny)
        remote(route.at[f], shelves.at[f], rs.at[k], rr.at[f], {"index": f}).wait_recv()

    for k in range(1, ny):
        route_copy(k).start()
    shelves[y] = route[y]

    for g in range(pieces):
        for here, there in edges:
            z_copy(g, here, there).wait_send()
    for d in (0,) + tuple(d for ds in order for d in ds):
        y_finish(d)
        if d:
            for which in range(2):
                x_copy(shifted(-d), which).wait_send()
                p_copy(shifted(-d), which).wait_send()
    for j in range(owned):
        for which in range(2):
            w_copy(j, which).wait_send()
            m_copy(j, which).wait_send()
    for pair in range(pairs):
        for which in range(2):
            halo(which, pair).wait_send()
        for k in (1, 3):
            c_copy(pair, k).wait_send()
            f_copy(pair, k).wait_send()
    for k in range(1, ns):
        pool_copy(k).wait_send()

    for k in range(1, ny):
        route_wait(k)
    found = jnp.concatenate([shelves[f, 0:per_block // 2] for f in range(ny)], axis=1)
    mean = jnp.sum(found * found, axis=1, keepdims=True) / (quarter * ny)
    shelf_ref[...] = found * lax.rsqrt(mean + 1e-6)
    for k in range(1, ny):
        route_copy(k).wait_send()


def body(hidden, proj_weight, stretch_lengths, shard_of):
    states = hidden[0]
    tokens, depth = states.shape
    pieces, rows, width = proj_weight.shape
    nz, ns, ny = (lax.axis_size(a) for a in ("dp", "seq", "index"))
    pairs = width // 128
    quarter = depth // ny
    slots = shard_of.shape[1] // 2
    dma = pltpu.SemaphoreType.DMA
    bf16, f32 = jnp.bfloat16, jnp.float32
    any_space = pl.BlockSpec(memory_space=pl.ANY)
    vmem_space = pl.BlockSpec(memory_space=VMEM)
    layer, shelf = pl.pallas_call(
        layer_kernel,
        out_shape=(jax.ShapeDtypeStruct((tokens, quarter), bf16), jax.ShapeDtypeStruct((slots, depth), f32)),
        in_specs=[pl.BlockSpec(memory_space=pltpu.SMEM), vmem_space, any_space, any_space],
        out_specs=[vmem_space] * 2,
        scratch_shapes=[
            VMEM((tokens, depth), bf16),
            VMEM((nz, 3, rows, width), bf16),
            VMEM((nz, rows // 4, width), bf16),
            VMEM((ny, nz // ny, rows, width), bf16),
            VMEM((3, tokens, width), f32),
            VMEM((pairs, tokens, 128), bf16),
            VMEM((pairs, 2, tokens, 128), bf16),
            VMEM((2, pairs, 2, tokens, 128), bf16),
            VMEM((ny, pairs, tokens, 128), bf16),
            VMEM((ns, 8, quarter), f32), VMEM((ns, 8, quarter), f32),
            VMEM((ny, 8, quarter), f32), VMEM((ny, 8, quarter), f32),
            dma((2,)),
            dma((pieces, nz - 1)), dma((pieces, nz)),
            dma((2, nz)), dma((2, nz)), dma((2, nz)), dma((2, nz)),
            dma((nz,)), dma((ny, nz // ny)), dma((nz // ny,)),
            dma((2, nz // ny)), dma((2, nz // ny)), dma((2, nz // ny)), dma((2, nz // ny)),
            dma((2, pairs)), dma((2, pairs)), dma((pairs, ny)), dma((pairs, ny)), dma((pairs, 2)), dma((pairs, 2)),
            dma((ns,)), dma((ns,)), dma((ny,)), dma((ny,)),
        ],
        compiler_params=pltpu.CompilerParams(collective_id=0, has_side_effects=True),
    )(shard_of[0, :, 0], stretch_lengths, states, proj_weight)
    return (layer[None], shelf[None, None, None])


def solution(mesh):
    in_specs = (P("dp", "seq", None), P(None, "dp", "index"), P("dp", None), P("dp", "seq", None))
    out_specs = (P("dp", "seq", "index"), P("dp", "seq", "index", None, None))
    return jax.shard_map(body, mesh=mesh, in_specs=in_specs, out_specs=out_specs, check_vma=False)
```

time: 227 us -> 79.8 us (0.35); the launches traced: 224 us -> 79.7 us
  waiting for transfers between devices: 136 us -> 0 us
  Pallas kernels: 0 us -> 76.8 us
  blocking collectives: 22.7 us -> 0 us
  starting transfers between devices: 20.5 us -> 0 us
  matrix products: 14.7 us -> 0 us
  between operations: 15 us -> 0.65 us
  other arithmetic: 7.88 us -> 0 us
  local copies, waits for them, and re-layouts: 7.61 us -> 2.28 us
    all_gather x1 -> x0, waiting for transfers between devices: 106 us -> none  [body(): shard_rows = lax.all_gather(proj_weight, 'dp', axis=1, tiled=True)]
    pallas_call x0 -> x1, Pallas kernels: none -> 76.8 us  [body(): pl.pallas_call(layer_kernel, out_shape=(jax.ShapeDtypeStruct((tokens, qua...]
    reduce_scatter x1 -> x0, waiting for transfers between devices: 22.7 us -> none  [body(): lax.psum_scatter(partial_value.astype(jnp.bfloat16), 'index', scatter_dim...]
    unnamed x1 -> x0, blocking collectives: 22.7 us -> none
    ppermute x2 -> x0, starting transfers between devices: 17.2 us -> none  [the longest x1 14.2 us: with_halo(): lax.ppermute(head, axis, [((i + 1) % count, i) for i in range(ends)])]
    dot_general x16 -> x0, matrix products: 14.7 us -> none  [the longest x1 4.08 us: body(): jnp.einsum('td,jdc->jtc', states, shard_rows[:3], preferred_element_type=...]
    ppermute x2 -> x0, waiting for transfers between devices: 4.65 us -> none  [the longest x1 3.47 us: with_halo(): lax.ppermute(head, axis, [((i + 1) % count, i) for i in range(ends)])]
    all_to_all x1 -> x0, starting transfers between devices: 3.25 us -> none  [body(): lax.all_to_all(outgoing, 'index', split_axis=0, concat_axis=2, tiled=True)]
  transfers between devices with their start and end apart: 5 -> 0, of which waited for: 5 -> 0; matrix products, arithmetic and copies ran while one was open for 3% -> 0% of each run, Pallas kernels for 0% -> 0%
where the time goes in v3:
time: 79.8 us; the launch traced here: 79.7 us
  Pallas kernels  76.8 us (96%)
  local copies, waits for them, and re-layouts  2.28 us (3%)
    pallas_call x1, Pallas kernels, body(): pl.pallas_call(layer_kernel, out_shape=(jax.ShapeDtypeStruct((tokens, qua...  76.8 us
    unnamed x4, local copies, waits for them, and re-layouts  2.28 us

profile of v3, /device:TPU:1, one launch (start us, length us, event | category | flops | bytes accessed | tf_op | source)
XLA Modules:
  0.0 79.7 jit_solution(17078901310567713434)
XLA Ops:
  0.6 76.8 %shard_map.59 = (bf16[256,512]{1,0:T(8,128)(2,1)}, f32[2,2048]{1,0:T(2,128)}) custom-call(s32[4]{0:T(128)} %bitcast.7, s32[1,32]{1,0:T(1,128)} %len_ref.1, bf16[256,2048]{1,0:T(8,128)(2,1)} %bitcast.4, bf16[4,128,384]{2,1,0:T(8,128)(2,1)} %w_hbm.1), custom_call_target="tpu_custom_call" | custom-call | tf_op jit(solution)/shard_map/pallas_call | solution.py:431
  77.4 0.0 copy-start
  77.4 1.7 %copy.8 = bf16[1,256,512]{2,1,0:T(8,128)(2,1)} copy(bf16[1,256,512]{2,1,0:T(8,128)(2,1)} %bitcast.5) | data formatting | bytes 524288
  79.1 0.0 copy-done
  79.1 0.6 copy.9
Async XLA Ops:
  77.4 1.7 %copy-start = (f32[2,2048]{1,0:T(2,128)S(1)}, f32[2,2048]{1,0:T(2,128)}, u32[]{:S(2)}) copy-start(f32[2,2048]{1,0:T(2,128)} %get-tuple-element.5) | copy-start | bytes 49156

commit v4 on v3

v4 whole, which is shorter than its diff:
```python
import jax
import jax.numpy as jnp
from jax import lax
from jax.experimental import pallas as pl
from jax.experimental.pallas import tpu as pltpu
from jax.sharding import PartitionSpec as P

HD = 64
MESH = pl.DeviceIdType.MESH
VMEM = pltpu.VMEM


def layer_kernel(shard_ref, len_ref, x_hbm, w_hbm, layer_ref, shelf_ref,
                 x_ref, near_x, w_all, w3_ring, w3, acc, near_acc, tables, queries, pair_kv, side, ctx,
                 id_send, id_all, member, send_rows, got,
                 local, zs, zr, xs, xr, ps, pr, ys, yr, yl, ws, wr, ms, mr,
                 ns_, nr, hs, hr, cs, cr, fs, fr, is_, ir, gs, gr):
    nz = lax.axis_size("dp")
    ns = lax.axis_size("seq")
    ny = lax.axis_size("index")
    z = lax.axis_index("dp")
    s = lax.axis_index("seq")
    y = lax.axis_index("index")
    pieces, rows, width = w_hbm.shape
    tokens = x_ref.shape[0]
    pairs = width // 128
    quarter = layer_ref.shape[1]
    owned = nz // ny
    core = lax.rem(s, 2)
    par = lax.rem(s // 2, 2)
    mate = {"seq": s + 1 - 2 * core}
    right = {"seq": lax.rem(s + 2, ns)}
    left = {"seq": lax.rem(s + ns - 2, ns)}
    near = s + 2 * core - 1
    neighbour = {"seq": lax.rem(near + ns, ns)}
    me = s * ny + y
    count = len_ref.shape[1]
    per_block = count // ns
    capacity = per_block // 2

    def remote(src, dst, send, recv, device):
        return pltpu.make_async_remote_copy(src_ref=src, dst_ref=dst, send_sem=send, recv_sem=recv,
                                            device_id=device, device_id_type=MESH)

    def shifted(d):
        return lax.rem(z + nz + d, nz)

    x_load = pltpu.make_async_copy(x_hbm, x_ref, local.at[0])
    x_load.start()
    own_load = pltpu.make_async_copy(w_hbm.at[pl.ds(0, 3)], w_all.at[z], local.at[1])
    own_load.start()

    barrier = pltpu.get_barrier_semaphore()
    for d in (1, -1):
        pl.semaphore_signal(barrier, inc=1, device_id={"dp": shifted(d)}, device_id_type=MESH)

    def greet(k, carry):
        t = lax.rem(me + k, ns * ny)
        pl.semaphore_signal(barrier, inc=1, device_id={"seq": t // ny, "index": lax.rem(t, ny)}, device_id_type=MESH)
        return carry

    lax.fori_loop(1, ns * ny, greet, 0)
    tile_row = lax.broadcasted_iota(jnp.int32, (8, 128), 0)
    ids = jnp.zeros((8, 128), jnp.int32)
    for i in range(per_block):
        ids = jnp.where(tile_row == i, shard_ref[i], ids)
    id_send[...] = ids
    id_all[s] = ids
    pl.semaphore_wait(barrier, ns * ny + 1)

    part = rows // 4
    sub = part // 2
    mine = pl.multiple_of(rows // 2 * par + part * core, 16)
    other = pl.multiple_of(rows // 2 * (1 - par) + part * core, 16)
    mate_mine = pl.multiple_of(rows // 2 * par + part * (1 - core), 16)
    mate_other = pl.multiple_of(rows // 2 * (1 - par) + part * (1 - core), 16)

    far = nz // 2
    edges = {}
    for d in range(far):
        for sign in ((1, -1) if d < far - 1 else (1,)):
            edges[sign * d, sign * (d + 1)] = len(edges)

    def z_ref(g, o):
        return w3_ring.at[o] if g == 3 else w_all.at[o, g, pl.ds(mine, part)]

    def z_copy(g, here, there):
        o = shifted(-here)
        dst = z_ref(g, o)
        src = w_hbm.at[g, pl.ds(mine, part)] if here == 0 else dst
        return remote(src, dst, zs.at[g, edges[here, there]], zr.at[g, o], {"dp": shifted(there - here)})

    def z_wait(g, d):
        o = shifted(-d)
        remote(z_ref(g, o), z_ref(g, o), zs.at[g, 0], zr.at[g, o], {"dp": shifted(1)}).wait_recv()

    def forward(g, d):
        for here, there in edges:
            if here == d:
                z_copy(g, here, there).start()

    def x_copy(o, which):
        ref = w_all.at[o, :, pl.ds(mine + which * sub, sub)]
        return remote(ref, ref, xs.at[which, o], xr.at[which, o], (right, left)[which])

    def x_wait(o, which):
        ref = w_all.at[o, :, pl.ds(other + which * sub, sub)]
        remote(ref, ref, xs.at[which, o], xr.at[which, o], right).wait_recv()

    def p_copy(o, which):
        ref = w_all.at[o, :, pl.ds((mine, other)[which], part)]
        return remote(ref, ref, ps.at[which, o], pr.at[which, o], mate)

    def p_wait(o, which):
        ref = w_all.at[o, :, pl.ds((mate_mine, mate_other)[which], part)]
        remote(ref, ref, ps.at[which, o], pr.at[which, o], mate).wait_recv()

    def y_local(d):
        o = shifted(-d)
        src = w_hbm.at[3, pl.ds(mine, part)] if d == 0 else w3_ring.at[o]
        j = lax.rem(o, owned)
        return pltpu.make_async_copy(src, w3.at[y, j, pl.ds(mine, part)], yl.at[j])

    def y_copy(d):
        o = shifted(-d)
        src = w_hbm.at[3, pl.ds(mine, part)] if d == 0 else w3_ring.at[o]
        j = lax.rem(o, owned)
        return remote(src, w3.at[y, j, pl.ds(mine, part)], ys.at[o], yr.at[y, j], {"index": o // owned})

    def y_start(d):
        stays = shifted(-d) // owned == y

        @pl.when(stays)
        def _():
            y_local(d).start()

        @pl.when(jnp.logical_not(stays))
        def _():
            y_copy(d).start()

    def y_finish(d):
        @pl.when(shifted(-d) // owned != y)
        def _():
            y_copy(d).wait_send()

    def w_copy(j, which):
        ref = w3.at[:, j, pl.ds(mine + which * sub, sub)]
        return remote(ref, ref, ws.at[which, j], wr.at[which, j], (right, left)[which])

    def w_wait(j, which):
        ref = w3.at[:, j, pl.ds(other + which * sub, sub)]
        remote(ref, ref, ws.at[which, j], wr.at[which, j], right).wait_recv()

    def m_copy(j, which):
        ref = w3.at[:, j, pl.ds((mine, other)[which], part)]
        return remote(ref, ref, ms.at[which, j], mr.at[which, j], mate)

    def m_wait(j, which):
        ref = w3.at[:, j, pl.ds((mate_mine, mate_other)[which], part)]
        remote(ref, ref, ms.at[which, j], mr.at[which, j], mate).wait_recv()

    def w_arrive(d):
        o = shifted(-d)
        j = lax.rem(o, owned)

        @pl.when(o // owned == y)
        def _():
            y_local(d).wait()
            for k in range(1, ny):
                f = lax.rem(y + k, ny)
                ref = w3.at[f, j, pl.ds(mine, part)]
                remote(ref, ref, ys.at[0], yr.at[f, j], {"index": f}).wait_recv()
            for which in range(2):
                w_copy(j, which).start()
            m_copy(j, 0).start()

    def w_cross(d):
        o = shifted(-d)
        j = lax.rem(o, owned)

        @pl.when(o // owned == y)
        def _():
            for which in range(2):
                w_wait(j, which)
            m_copy(j, 1).start()

    def beside(k):
        return {"index": lax.rem(y + k, ny)}

    share = tokens // ny

    def n_rows(k, lower_half=None):
        f = lax.rem(y + k, ny)
        if lower_half is None:
            return near_x.at[pl.ds(pl.multiple_of(f * share, share), share)]
        start = f * share + (0 if lower_half else share // 2)
        return near_x.at[pl.ds(pl.multiple_of(start, share // 2), share // 2)]

    def n_first():
        src = x_hbm.at[pl.ds(pl.multiple_of(y * share, share), share)]
        return remote(src, n_rows(0), ns_.at[0], nr.at[0], neighbour)

    def n_copy(k):
        return remote(n_rows(0), n_rows(0), ns_.at[k], nr.at[4 - k], beside(k))

    def n_wait(k):
        remote(n_rows(k), n_rows(k), ns_.at[k], nr.at[k], beside(k)).wait_recv()

    def n_relay(k):
        ref = n_rows(k, k == 3)
        return remote(ref, ref, ns_.at[3 + k], nr.at[3 + k], beside(ny - k))

    def n_relay_wait(k):
        ref = n_rows(2, k == 3)
        remote(ref, ref, ns_.at[3 + k], nr.at[3 + k], beside(k)).wait_recv()

    def i_copy(k):
        t = lax.rem(s + k, ns)
        return remote(id_send, id_all.at[s], is_.at[k], ir.at[s], {"seq": t})

    for g in range(pieces):
        forward(g, 0)
    y_start(0)
    n_first().start()
    for k in range(1, ns):
        i_copy(k).start()

    half = HD // 2
    lane = lax.broadcasted_iota(jnp.int32, (tokens, 128), 1)
    lower = lax.rem(lane, HD) < half
    freqs = jnp.exp(lax.rem(lane, half).astype(jnp.float32) * (-2.0 / HD * 9.210340371976184))
    token = lax.broadcasted_iota(jnp.int32, (tokens, 128), 0)

    def fill_tables(i, block):
        angles = (token + block * tokens).astype(jnp.float32) * freqs
        tables[2 * i] = jnp.cos(angles)
        sine = jnp.sin(angles)
        tables[2 * i + 1] = jnp.where(lower, -sine, sine)


    def arrive(ds):
        for d in ds:
            for g in range(3):
                z_wait(g, d)
                forward(g, d)
            for which in range(2):
                x_copy(shifted(-d), which).start()
            p_copy(shifted(-d), 0).start()
        for d in ds:
            z_wait(3, d)
            forward(3, d)
            y_start(d)

    def cross(ds):
        for d in ds:
            for which in range(2):
                x_wait(shifted(-d), which)
            p_copy(shifted(-d), 1).start()

    def lhs_of(ref, ds):
        return jnp.concatenate([ref[:, pl.ds(pl.multiple_of(o * rows, 128), rows)] for o in origins(ds)], axis=1)

    def origins(ds):
        return [shifted(-d) for d in (ds if len(ds) == 2 else (0, ds[0]))]

    def rhs_of(j, ds):
        return jnp.concatenate([w_all[o, j] for o in origins(ds)], axis=0)

    def near_multiply(ds, first):
        lhs = lhs_of(near_x, ds)
        for j in (1, 2):
            product = jnp.dot(lhs, rhs_of(j, ds), preferred_element_type=jnp.float32)
            near_acc[j - 1] = product if first else near_acc[j - 1] + product

    def settle(ds, first, both):
        for d in ds:
            for which in range(2):
                p_wait(shifted(-d), which)
        lhs = lhs_of(x_ref, ds)
        product = jnp.dot(lhs, rhs_of(0, ds), preferred_element_type=jnp.float32)
        acc[0] = product if first else acc[0] + product
        if both:
            lhs = jnp.concatenate([lhs, lhs_of(near_x, ds)], axis=0)
        for j in (1, 2):
            product = jnp.dot(lhs, rhs_of(j, ds), preferred_element_type=jnp.float32)
            acc[j] = product[:tokens] if first else acc[j] + product[:tokens]
            if both:
                near_acc[j - 1] += product[tokens:]

    def place_stretches():
        for k in range(1, ns):
            f = lax.rem(s + k, ns)
            remote(id_all.at[f], id_all.at[f], is_.at[k], ir.at[f], {"seq": f}).wait_recv()
        slots = ns * 8
        slot = lax.broadcasted_iota(jnp.int32, (slots, count), 0)
        stretch = lax.rem(slot, 8) * ns + slot // 8
        which_stretch = lax.broadcasted_iota(jnp.int32, (slots, count), 1)
        lengths = jnp.broadcast_to(len_ref[...], (slots, count))
        cube = (ns, 8, 128)

        def wide(picked):
            return jnp.broadcast_to(jnp.sum(jnp.where(picked, lengths, 0), axis=1, keepdims=True), (slots, 128)).reshape(cube)

        ends = wide(which_stretch <= stretch)
        starts = wide(which_stretch < stretch)
        line = lax.broadcasted_iota(jnp.int32, cube, 1)
        shard = id_all[...]

        def spread(value, i):
            return jnp.broadcast_to(value[:, i:i + 1, :], cube)

        rank = jnp.zeros(cube, jnp.int32)
        for i in range(per_block - 1):
            rank += jnp.where(jnp.logical_and(spread(shard, i) == shard, line > i), 1, 0)
        place = shard * capacity + rank
        first = jnp.zeros(cube, jnp.int32)
        last = jnp.zeros(cube, jnp.int32)
        for i in range(per_block):
            here = spread(place, i) == line
            first = jnp.where(here, spread(starts, i), first)
            last = jnp.where(here, spread(ends, i), last)
        first, last = first.reshape(slots, 128), last.reshape(slots, 128)
        for start in range(0, tokens, 128):
            position = lax.broadcasted_iota(jnp.int32, (slots, 128), 1) + (s * tokens + start)
            inside = jnp.logical_and(position >= first, position < last)
            member[:, start:start + 128] = jnp.where(inside, 1.0, 0.0).astype(jnp.bfloat16)

    order = [(d, -d) for d in range(1, far)] + [(far,)]
    turns = len(order) + 2
    for i in range(turns):
        if i < len(order):
            arrive(order[i])
        if 1 <= i <= len(order):
            cross(order[i - 1])
        if i == 1:
            n_first().wait_recv()
            for k in (1, 3):
                n_copy(k).start()
            x_load.wait()
            own_load.wait()
        if i == 2:
            place_stretches()
        if i == 3:
            fill_tables(0, s)
        if i == 4:
            for k in (1, 3):
                n_wait(k)
                n_relay(k).start()
        if i == 5:
            fill_tables(1, near)
        if i == 6:
            for k in (1, 3):
                n_relay_wait(k)
        if i in (6, 7):
            for m in (2 * i - 12, 2 * i - 11):
                near_multiply(order[m], m == 0)
        if i >= 2:
            settle(order[i - 2], i == 2, i >= 6)
        if i >= 4:
            for d in order[i - 4] + ((0,) if i == 4 else ()):
                w_arrive(d)
        if i >= 6:
            for d in order[i - 6] + ((0,) if i == 6 else ()):
                w_cross(d)

    def turned(value, i):
        swapped = jnp.where(lower, pltpu.roll(value, 128 - half, 1), pltpu.roll(value, half, 1))
        return value * tables[2 * i] + swapped * tables[2 * i + 1]

    def h_copy(pair):
        return remote(pair_kv.at[pair], side.at[core, pair], hs.at[pair], hr.at[pair], mate)

    def h_wait(pair):
        ref = side.at[1 - core, pair]
        remote(ref, ref, hs.at[pair], hr.at[pair], mate).wait_recv()

    blocks = [slice(pair * 128, pair * 128 + 128) for pair in range(pairs)]
    for pair, cols in enumerate(blocks):
        pair_kv[pair, 0] = turned(acc[1, :, cols], 0).astype(jnp.bfloat16)
        pair_kv[pair, 1] = acc[2, :, cols].astype(jnp.bfloat16)
        h_copy(pair).start()
    for pair, cols in enumerate(blocks):
        side[core, pair, 0] = turned(near_acc[0, :, cols], 1).astype(jnp.bfloat16)
        side[core, pair, 1] = near_acc[1, :, cols].astype(jnp.bfloat16)
        queries[pair] = (turned(acc[0, :, cols], 0) * HD ** -0.5).astype(jnp.bfloat16)

    for ds in order[turns - 4:]:
        for d in ds:
            w_arrive(d)

    strip = tokens // 2

    def c_rows(f, piece, start=0, size=strip):
        return ctx.at[f, piece // 2, pl.ds(piece % 2 * strip + start, size)]

    def c_copy(piece, k):
        ref = c_rows(y, piece)
        return remote(ref, ref, cs.at[piece, k], cr.at[piece, y], beside(k))

    def c_wait(piece, k):
        f = lax.rem(y + k, ny)
        ref = c_rows(f, piece)
        remote(ref, ref, cs.at[piece, k], cr.at[piece, f], beside(k)).wait_recv()

    def f_copy(piece, k):
        ref = c_rows(lax.rem(y + k, ny), piece, 0 if k == 3 else strip // 2, strip // 2)
        return remote(ref, ref, fs.at[piece, k // 2], fr.at[piece, k // 2], beside(ny - k))

    def f_wait(piece, k):
        ref = c_rows(lax.rem(y + 2, ny), piece, 0 if k == 3 else strip // 2, strip // 2)
        remote(ref, ref, fs.at[piece, k // 2], fr.at[piece, k // 2], beside(k)).wait_recv()

    def relay(piece):
        for k in (1, 3):
            c_wait(piece, k)
            f_copy(piece, k).start()

    def scores(query, key):
        return lax.dot_general(query, key, (((1,), (1,)), ((), ())), preferred_element_type=jnp.float32)

    lag = 4
    narrow = lax.broadcasted_iota(jnp.int32, (strip, 128), 1)
    for pair in range(pairs):
        h_wait(pair)
        for part_of in range(2):
            piece = 2 * pair + part_of
            top_row = part_of * strip
            query = queries[pair, top_row:top_row + strip]
            low_keys = slice(top_row, tokens)
            high_keys = slice(0, top_row + strip)
            low_shape = (strip, tokens - top_row)
            high_shape = (strip, top_row + strip)
            see_low = jnp.logical_and(lax.broadcasted_iota(jnp.int32, low_shape, 1) >= lax.broadcasted_iota(jnp.int32, low_shape, 0), s > 0)
            see_high = jnp.logical_and(
                lax.broadcasted_iota(jnp.int32, high_shape, 1) <= lax.broadcasted_iota(jnp.int32, high_shape, 0) + top_row, s < ns - 1)
            results = []
            for head in range(2):
                inside = (narrow < HD) if head == 0 else (narrow >= HD)
                chosen = jnp.where(inside, query, jnp.zeros_like(query))
                low = jnp.where(see_low, scores(chosen, side[0, pair, 0, low_keys]), -1e30)
                mid = scores(chosen, pair_kv[pair, 0])
                high = jnp.where(see_high, scores(chosen, side[1, pair, 0, high_keys]), -1e30)
                top = jnp.maximum(jnp.max(mid, axis=1, keepdims=True), jnp.maximum(
                    jnp.max(low, axis=1, keepdims=True), jnp.max(high, axis=1, keepdims=True)))
                low, mid, high = jnp.exp(low - top), jnp.exp(mid - top), jnp.exp(high - top)
                total = (jnp.sum(low, axis=1, keepdims=True) + jnp.sum(mid, axis=1, keepdims=True)
                         + jnp.sum(high, axis=1, keepdims=True))
                value = jnp.dot(low.astype(jnp.bfloat16), side[0, pair, 1, low_keys], preferred_element_type=jnp.float32)
                value += jnp.dot(mid.astype(jnp.bfloat16), pair_kv[pair, 1], preferred_element_type=jnp.float32)
                value += jnp.dot(high.astype(jnp.bfloat16), side[1, pair, 1, high_keys], preferred_element_type=jnp.float32)
                results.append(value / total)
            ctx[y, pair, top_row:top_row + strip] = jnp.where(narrow < HD, results[0], results[1]).astype(jnp.bfloat16)
            for k in (1, 3):
                c_copy(piece, k).start()
            if piece >= lag:
                relay(piece - lag)
            if piece == 2:
                for ds in order[turns - 6:]:
                    for d in ds:
                        w_cross(d)

    def project(k):
        f = lax.rem(y + k, ny)
        context = jnp.concatenate([ctx[f, pair] for pair in range(pairs)], axis=1)
        return jnp.concatenate([scores(context, w3[f, j]) for j in range(owned)], axis=1)

    for j in range(owned):
        for which in range(2):
            m_wait(j, which)
    summed = x_ref[:, pl.ds(pl.multiple_of(y * quarter, 128), quarter)].astype(jnp.float32) + project(0)
    for piece in range(2 * pairs - lag, 2 * pairs):
        relay(piece)
    summed += project(1)
    summed += project(3)
    for piece in range(2 * pairs):
        for k in (1, 3):
            f_wait(piece, k)
    summed += project(2)
    layer = summed.astype(jnp.bfloat16)
    layer_ref[...] = layer

    partial = jnp.dot(member[...], layer, preferred_element_type=jnp.float32)
    for t in range(ns * ny):
        send_rows[t] = partial[t * capacity:(t + 1) * capacity]

    def g_copy(k):
        t = lax.rem(me + k, ns * ny)
        return remote(send_rows.at[t], got.at[me], gs.at[t], gr.at[me], {"seq": t // ny, "index": lax.rem(t, ny)})

    def g_start(k, carry):
        g_copy(k).start()
        return carry

    lax.fori_loop(1, ns * ny, g_start, 0)
    got[me] = send_rows[me]

    for g in range(pieces):
        for here, there in edges:
            z_copy(g, here, there).wait_send()
    for d in (0,) + tuple(d for ds in order for d in ds):
        y_finish(d)
        if d:
            for which in range(2):
                x_copy(shifted(-d), which).wait_send()
                p_copy(shifted(-d), which).wait_send()
    for j in range(owned):
        for which in range(2):
            w_copy(j, which).wait_send()
            m_copy(j, which).wait_send()
    n_first().wait_send()
    for k in (1, 3):
        n_copy(k).wait_send()
        n_relay(k).wait_send()
    for pair in range(pairs):
        h_copy(pair).wait_send()
    for piece in range(2 * pairs):
        for k in (1, 3):
            c_copy(piece, k).wait_send()
            f_copy(piece, k).wait_send()
    for k in range(1, ns):
        i_copy(k).wait_send()

    def g_finish(k, carry):
        t = lax.rem(me + k, ns * ny)
        remote(send_rows.at[t], got.at[t], gs.at[t], gr.at[t], {"seq": t // ny, "index": lax.rem(t, ny)}).wait()
        return carry

    lax.fori_loop(1, ns * ny, g_finish, 0)
    parts = []
    for f in range(ny):
        part_sum = got[f]
        for t in range(1, ns):
            part_sum += got[t * ny + f]
        parts.append(part_sum)
    found = jnp.concatenate(parts, axis=1)
    mean = jnp.sum(found * found, axis=1, keepdims=True) / (quarter * ny)
    shelf_ref[...] = found * lax.rsqrt(mean + 1e-6)


def body(hidden, proj_weight, stretch_lengths, shard_of):
    states = hidden[0]
    tokens, depth = states.shape
    pieces, rows, width = proj_weight.shape
    nz, ns, ny = (lax.axis_size(a) for a in ("dp", "seq", "index"))
    pairs = width // 128
    quarter = depth // ny
    slots = shard_of.shape[1] // 2
    dma = pltpu.SemaphoreType.DMA
    bf16, f32 = jnp.bfloat16, jnp.float32
    any_space = pl.BlockSpec(memory_space=pl.ANY)
    vmem_space = pl.BlockSpec(memory_space=VMEM)
    layer, shelf = pl.pallas_call(
        layer_kernel,
        out_shape=(jax.ShapeDtypeStruct((tokens, quarter), bf16), jax.ShapeDtypeStruct((slots, depth), f32)),
        in_specs=[pl.BlockSpec(memory_space=pltpu.SMEM), vmem_space, any_space, any_space],
        out_specs=[vmem_space] * 2,
        scratch_shapes=[
            VMEM((tokens, depth), bf16), VMEM((tokens, depth), bf16),
            VMEM((nz, 3, rows, width), bf16),
            VMEM((nz, rows // 4, width), bf16),
            VMEM((ny, nz // ny, rows, width), bf16),
            VMEM((3, tokens, width), f32), VMEM((2, tokens, width), f32),
            VMEM((4, tokens, 128), f32),
            VMEM((pairs, tokens, 128), bf16),
            VMEM((pairs, 2, tokens, 128), bf16),
            VMEM((2, pairs, 2, tokens, 128), bf16),
            VMEM((ny, pairs, tokens, 128), bf16),
            VMEM((8, 128), jnp.int32), VMEM((ns, 8, 128), jnp.int32),
            VMEM((ns * 8, tokens), bf16),
            VMEM((ns * ny, slots, quarter), f32), VMEM((ns * ny, slots, quarter), f32),
            dma((2,)),
            dma((pieces, nz - 1)), dma((pieces, nz)),
            dma((2, nz)), dma((2, nz)), dma((2, nz)), dma((2, nz)),
            dma((nz,)), dma((ny, nz // ny)), dma((nz // ny,)),
            dma((2, nz // ny)), dma((2, nz // ny)), dma((2, nz // ny)), dma((2, nz // ny)),
            dma((7,)), dma((7,)),
            dma((pairs,)), dma((pairs,)),
            dma((2 * pairs, ny)), dma((2 * pairs, ny)), dma((2 * pairs, 2)), dma((2 * pairs, 2)),
            dma((ns,)), dma((ns,)), dma((ns * ny,)), dma((ns * ny,)),
        ],
        compiler_params=pltpu.CompilerParams(collective_id=0, has_side_effects=True),
    )(shard_of[0, :, 0], stretch_lengths, states, proj_weight)
    return (layer[None], shelf[None, None, None])


def solution(mesh):
    in_specs = (P("dp", "seq", None), P(None, "dp", "index"), P("dp", None), P("dp", "seq", None))
    out_specs = (P("dp", "seq", "index"), P("dp", "seq", "index", None, None))
    return jax.shard_map(body, mesh=mesh, in_specs=in_specs, out_specs=out_specs, check_vma=False)
```

time: 79.8 us -> 76.8 us (0.962)
  Pallas kernels: 76.8 us -> 73.7 us
    pallas_call x1, Pallas kernels: 76.8 us -> 73.7 us  [body(): pl.pallas_call(layer_kernel, out_shape=(jax.ShapeDtypeStruct((tokens, qua...]
where the time goes in v4:
time: 76.8 us; the launch traced here: 76.6 us
  Pallas kernels  73.7 us (96%)
  local copies, waits for them, and re-layouts  2.28 us (3%)
    pallas_call x1, Pallas kernels, body(): pl.pallas_call(layer_kernel, out_shape=(jax.ShapeDtypeStruct((tokens, qua...  73.7 us
    unnamed x4, local copies, waits for them, and re-layouts  2.28 us

profile of v4, /device:TPU:1, one launch (start us, length us, event | category | flops | bytes accessed | tf_op | source)
XLA Modules:
  0.0 76.6 jit_solution(8206824735994159085)
XLA Ops:
  0.6 73.7 %shard_map.59 = (bf16[256,512]{1,0:T(8,128)(2,1)}, f32[2,2048]{1,0:T(2,128)}) custom-call(s32[4]{0:T(128)} %bitcast.7, s32[1,32]{1,0:T(1,128)} %len_ref.1, bf16[256,2048]{1,0:T(8,128)(2,1)} %bitcast.4, bf16[4,128,384]{2,1,0:T(8,128)(2,1)} %w_hbm.1), custom_call_target="tpu_custom_call" | custom-call | tf_op jit(solution)/shard_map/pallas_call | solution.py:552
  74.3 0.0 copy-start
  74.4 1.7 %copy.8 = bf16[1,256,512]{2,1,0:T(8,128)(2,1)} copy(bf16[1,256,512]{2,1,0:T(8,128)(2,1)} %bitcast.5) | data formatting | bytes 524288
  76.0 0.0 copy-done
  76.0 0.6 copy.9
Async XLA Ops:
  74.3 1.7 %copy-start = (f32[2,2048]{1,0:T(2,128)S(1)}, f32[2,2048]{1,0:T(2,128)}, u32[]{:S(2)}) copy-start(f32[2,2048]{1,0:T(2,128)} %get-tuple-element.5) | copy-start | bytes 49156

commit v5 on v4

--- a/solution.py
+++ b/solution.py
@@ -10,9 +10,9 @@
 VMEM = pltpu.VMEM
 
 
-def layer_kernel(shard_ref, len_ref, x_hbm, w_hbm, layer_ref, shelf_ref,
+def layer_kernel(shard_hbm, len_hbm, x_hbm, w_hbm, layer_ref, shelf_ref,
                  x_ref, near_x, w_all, w3_ring, w3, acc, near_acc, tables, queries, pair_kv, side, ctx,
-                 id_send, id_all, member, send_rows, got,
+                 shard_ref, len_ref, id_send, id_all, member, send_rows, got,
                  local, zs, zr, xs, xr, ps, pr, ys, yr, yl, ws, wr, ms, mr,
                  ns_, nr, hs, hr, cs, cr, fs, fr, is_, ir, gs, gr):
     nz = lax.axis_size("dp")
@@ -34,7 +34,7 @@
     near = s + 2 * core - 1
     neighbour = {"seq": lax.rem(near + ns, ns)}
     me = s * ny + y
-    count = len_ref.shape[1]
+    count = len_hbm.shape[1]
     per_block = count // ns
     capacity = per_block // 2
 
@@ -46,20 +46,24 @@
         return lax.rem(z + nz + d, nz)
 
     x_load = pltpu.make_async_copy(x_hbm, x_ref, local.at[0])
+    shard_load = pltpu.make_async_copy(shard_hbm, shard_ref, local.at[2])
+    shard_load.start()
+    len_load = pltpu.make_async_copy(len_hbm, len_ref, local.at[3])
+    len_load.start()
     x_load.start()
     own_load = pltpu.make_async_copy(w_hbm.at[pl.ds(0, 3)], w_all.at[z], local.at[1])
     own_load.start()
 
     barrier = pltpu.get_barrier_semaphore()
+    far_first = sorted(((a, b) for a in range(ns) for b in range(ny) if a or b),
+                       key=lambda p: -min(p[0] // 2, (ns - p[0]) // 2) - min(p[1], ny - p[1]))
+    for a, b in far_first:
+        pl.semaphore_signal(barrier, inc=1, device_id={"seq": lax.rem(s + a, ns), "index": lax.rem(y + b, ny)},
+                            device_id_type=MESH)
     for d in (1, -1):
         pl.semaphore_signal(barrier, inc=1, device_id={"dp": shifted(d)}, device_id_type=MESH)
-
-    def greet(k, carry):
-        t = lax.rem(me + k, ns * ny)
-        pl.semaphore_signal(barrier, inc=1, device_id={"seq": t // ny, "index": lax.rem(t, ny)}, device_id_type=MESH)
-        return carry
-
-    lax.fori_loop(1, ns * ny, greet, 0)
+    shard_load.wait()
+    len_load.wait()
     tile_row = lax.broadcasted_iota(jnp.int32, (8, 128), 0)
     ids = jnp.zeros((8, 128), jnp.int32)
     for i in range(per_block):
@@ -552,7 +556,7 @@
     layer, shelf = pl.pallas_call(
         layer_kernel,
         out_shape=(jax.ShapeDtypeStruct((tokens, quarter), bf16), jax.ShapeDtypeStruct((slots, depth), f32)),
-        in_specs=[pl.BlockSpec(memory_space=pltpu.SMEM), vmem_space, any_space, any_space],
+        in_specs=[any_space] * 4,
         out_specs=[vmem_space] * 2,
         scratch_shapes=[
             VMEM((tokens, depth), bf16), VMEM((tokens, depth), bf16),
@@ -565,10 +569,11 @@
             VMEM((pairs, 2, tokens, 128), bf16),
             VMEM((2, pairs, 2, tokens, 128), bf16),
             VMEM((ny, pairs, tokens, 128), bf16),
+            pltpu.SMEM((shard_of.shape[1],), jnp.int32), VMEM((1, stretch_lengths.shape[1]), jnp.int32),
             VMEM((8, 128), jnp.int32), VMEM((ns, 8, 128), jnp.int32),
             VMEM((ns * 8, tokens), bf16),
             VMEM((ns * ny, slots, quarter), f32), VMEM((ns * ny, slots, quarter), f32),
-            dma((2,)),
+            dma((4,)),
             dma((pieces, nz - 1)), dma((pieces, nz)),
             dma((2, nz)), dma((2, nz)), dma((2, nz)), dma((2, nz)),
             dma((nz,)), dma((ny, nz // ny)), dma((nz // ny,)),

time: 76.8 us -> 75.9 us (0.988)
  Pallas kernels: 73.7 us -> 72.9 us
    pallas_call x1, Pallas kernels: 73.7 us -> 72.9 us  [body(): pl.pallas_call(layer_kernel, out_shape=(jax.ShapeDtypeStruct((tokens, qua...]
where the time goes in v5:
time: 75.9 us; the launch traced here: 75.8 us
  Pallas kernels  72.9 us (96%)
  local copies, waits for them, and re-layouts  2.28 us (3%)
    pallas_call x1, Pallas kernels, body(): pl.pallas_call(layer_kernel, out_shape=(jax.ShapeDtypeStruct((tokens, qua...  72.9 us
    unnamed x4, local copies, waits for them, and re-layouts  2.28 us

profile of v5, /device:TPU:1, one launch (start us, length us, event | category | flops | bytes accessed | tf_op | source)
XLA Modules:
  0.0 75.8 jit_solution(1843363078753365888)
XLA Ops:
  0.6 72.9 %shard_map.59 = (bf16[256,512]{1,0:T(8,128)(2,1)}, f32[2,2048]{1,0:T(2,128)}) custom-call(s32[4]{0:T(128)} %bitcast.7, s32[1,32]{1,0:T(1,128)} %len_hbm.1, bf16[256,2048]{1,0:T(8,128)(2,1)} %bitcast.4, bf16[4,128,384]{2,1,0:T(8,128)(2,1)} %w_hbm.1), custom_call_target="tpu_custom_call" | custom-call | tf_op jit(solution)/shard_map/pallas_call | solution.py:556
  73.5 0.0 copy-start
  73.5 1.7 %copy.8 = bf16[1,256,512]{2,1,0:T(8,128)(2,1)} copy(bf16[1,256,512]{2,1,0:T(8,128)(2,1)} %bitcast.5) | data formatting | bytes 524288
  75.2 0.0 copy-done
  75.2 0.6 copy.9
Async XLA Ops:
  73.5 1.7 %copy-start = (f32[2,2048]{1,0:T(2,128)S(1)}, f32[2,2048]{1,0:T(2,128)}, u32[]{:S(2)}) copy-start(f32[2,2048]{1,0:T(2,128)} %get-tuple-element.5) | copy-start | bytes 49156
